TPU v7x, 256 devices: a whole 4x4x8 slice. The times are simulated.
256 devices in a mesh: chan: 64 (over y, z, core), hour: 4 (over x).
Axes of the slice: x: 4, y: 4, z: 8, core: 2. Of those that a mesh axis runs over, the one named last changes fastest.
Arguments:
- spectra: bfloat16 [8, 2, 8192, 2560], P('hour', None, 'chan'), may hold values from -34 to 34, as said below
- partner_lists: int32 [64, 4], replicated, may hold values from -1 to 63, as said below
- partner_counts: int32 [64], replicated, may hold values from 2 to 4, as said below
Outputs:
- stacks: float32 [256, 8, 128, 256], P(('chan', 'hour'))
Inputs may be any that keep to these rules, and one draw needn't show every extreme that they name: The spectra are finite and bounded. `partner_lists`: row s lists distinct channel blocks, the first being s itself; entries from position partner_counts[s] on are -1. Within their counts, every block is listed by at most 4 rows, and some block by exactly 4. `partner_counts`: some row has exactly 4 partners.
All inputs are finite; a program needn't handle non-finite values.
Results may differ from a plain program's by a relative error of at most 0.0046.
Values may be sent and summed in bfloat16 or wider, within the bound.
A program may use at most 128 MiB of HBM per device.

v0:
```python
import math

import jax
import jax.numpy as jnp
from jax import lax
from jax.sharding import PartitionSpec as P

VS = 8
F0 = 64
NWIN = 8192
SMOOTH = 129
LAGS = 256


def whiten(real_part, imag_part):
    amplitude = jnp.sqrt(real_part * real_part + imag_part * imag_part)
    window_shape = (1,) * (amplitude.ndim - 1) + (SMOOTH,)
    padding = ((0, 0),) * (amplitude.ndim - 1) + ((SMOOTH // 2, SMOOTH // 2),)
    summed = lax.reduce_window(
        amplitude,
        jnp.zeros((), amplitude.dtype),
        lax.add,
        window_shape,
        (1,) * amplitude.ndim,
        padding,
    )
    denominator = summed / SMOOTH + 1e-06
    return (
        (real_part / denominator).astype(jnp.bfloat16),
        (imag_part / denominator).astype(jnp.bfloat16),
    )


def lag_table(band_bins):
    freq_index = jnp.arange(band_bins, dtype=jnp.int32)[:, None] + F0
    lag_index = jnp.arange(LAGS, dtype=jnp.int32)[None, :] - LAGS // 2
    lag_index = jnp.where(lag_index < 0, lag_index + NWIN, lag_index)
    phase_index = freq_index * lag_index % NWIN
    phase_angle = phase_index.astype(jnp.float32) * (2.0 * math.pi / NWIN)
    return jnp.concatenate([jnp.cos(phase_angle), -jnp.sin(phase_angle)], 0).astype(jnp.bfloat16)


def slot_onehot(partner_lists, partner_counts, receiver):
    offsets = jnp.arange(partner_lists.shape[1], dtype=jnp.int32)
    listed = (offsets[None, :] < partner_counts[:, None]) & (partner_lists == receiver)
    member = jnp.any(listed, axis=1)
    slot_rank = jnp.cumsum(member.astype(jnp.int32)) - 1
    slots = jnp.arange(partner_lists.shape[1], dtype=jnp.int32)
    return member[None, :] & (slot_rank[None, :] == slots[:, None])


def shards(spectra, partner_lists, partner_counts):
    windows, _, block_chans, band_bins = spectra.shape
    block_count = lax.axis_size("chan")
    hour_count = lax.axis_size("hour")
    values = spectra.astype(jnp.float32)
    white_re, white_im = whiten(values[:, 0], values[:, 1])
    stride = block_chans // VS
    local_sources = jnp.stack([white_re[:, ::stride, :], white_im[:, ::stride, :]], 1)
    local_sources = jnp.transpose(local_sources, (2, 0, 1, 3))
    receiver = lax.axis_index("chan")
    onehot = slot_onehot(partner_lists, partner_counts, receiver).astype(jnp.bfloat16)
    slot_total = onehot.shape[0]
    gathered = lax.all_gather(local_sources, "chan", axis=0, tiled=True)
    flattened = gathered.reshape(block_count, -1)
    chosen = jnp.dot(onehot, flattened, preferred_element_type=jnp.float32)
    chosen = chosen.reshape(slot_total, VS, windows, 2, band_bins)
    table_values = lag_table(band_bins)
    norm_scale = 1.0 / math.sqrt(4.0 * band_bins * windows * hour_count)

    def one_slot(source):
        cross_re = jnp.zeros((VS, block_chans, band_bins), jnp.float32)
        cross_im = jnp.zeros((VS, block_chans, band_bins), jnp.float32)
        for window in range(windows):
            src_real = source[:, window, 0][:, None, :]
            src_imag = source[:, window, 1][:, None, :]
            recv_real = white_re[window][None, :, :]
            recv_imag = white_im[window][None, :, :]
            cross_re = cross_re + src_real * recv_real + src_imag * recv_imag
            cross_im = cross_im + src_imag * recv_real - src_real * recv_imag
        cross = (
            jnp.concatenate([cross_re, cross_im], -1)
            .astype(jnp.bfloat16)
            .reshape(VS * block_chans, 2 * band_bins)
        )
        lagged = jnp.dot(cross, table_values, preferred_element_type=jnp.float32) * norm_scale
        return lagged.reshape(VS, block_chans, LAGS)

    partial_stacks = lax.map(one_slot, chosen)
    summed_hours = lax.psum(partial_stacks, "hour")
    share = slot_total // hour_count
    return lax.dynamic_slice_in_dim(summed_hours, lax.axis_index("hour") * share, share, 0)


def solution(mesh):
    return jax.shard_map(
        shards,
        mesh=mesh,
        in_specs=(P("hour", None, "chan", None), P(), P()),
        out_specs=P(("chan", "hour"), None, None, None),
        check_vma=False,
    )
```

profile of v0, /device:TPU:1, one launch (start us, length us, event | category | flops | bytes accessed | tf_op | source)
XLA Modules:
  0.0 464.1 jit_solution(17760751546049418316)
XLA Ops:
  6.5 0.0 all-gather.2.cloned.1.call-start
  6.5 3.2 copy.26
  9.8 0.3 convert_element_type.43
  10.1 0.0 copy-start
  10.1 2.3 copy-done
  12.4 0.8 add_sqrt_fusion
  13.3 129.2 %reduce_window.7 = f32[2,128,2560]{1,2,0:T(8,128)} reduce-window(f32[2,128,2560]{1,2,0:T(8,128)S(1)} %add_sqrt_fusion, f32[]{:T(128)} %constant.29.clone.1), window={size=1x1x129 pad=0_0x0_0x64_64}, to_apply=%region_2.0 | reduce-window | flops 83886080 | bytes 5242884 | tf_op jit(solution)/shard_map/reduce_window | solution.py:19
  142.4 4.0 divide_convert_fusion.1
  146.4 0.0 copy-start.1
  146.4 10.4 %slice.38 = bf16[2,8,2560]{1,2,0:T(8,128)(2,1)} slice(bf16[2,128,2560]{1,2,0:T(8,128)(2,1)S(1)} %get-tuple-element.90), slice={[0:2:1], [0:128:16], [0:2560:1]} | slice | bytes 163840 | tf_op jit(solution)/shard_map/slice | solution.py:59
  156.8 10.2 %slice.39 = bf16[2,8,2560]{1,2,0:T(8,128)(2,1)} slice(bf16[2,128,2560]{1,2,0:T(8,128)(2,1)S(1)} %get-tuple-element.91), slice={[0:2:1], [0:128:16], [0:2560:1]} | slice | bytes 163840 | tf_op jit(solution)/shard_map/slice | solution.py:59
  167.0 0.0 copy-done.1
  167.0 3.8 maximum_bitcast_fusion
  170.8 3.5 copy.27
  174.4 0.0 all-gather.2.cloned.1.call-update
  174.4 0.0 all-reduce.2.cloned.1.call-start
  174.4 0.0 copy-start.3
  174.4 0.0 copy-start.4
  174.5 0.6 copy.30
  175.1 1.6 copy.31
  176.8 0.1 copy.25
  176.9 0.1 reduce-window.8
  177.0 0.1 add_reduce_fusion
  177.1 11.7 %cosine_convert_fusion = (bf16[2560,256]{1,0:T(8,128)(2,1)S(1)}, bf16[2560,256]{1,0:T(8,128)(2,1)S(1)}) fusion(s32[256]{0:T(256)S(1)} %compare_select_fusion, s32[2560]{0:T(1024)S(1)} %iota_add_fusion), kind=kLoop, calls=%fused_computation.34 | loop fusion | flops 11141120 | bytes 2632704 | tf_op jit(solution)/shard_map/convert.9
  188.8 1.7 pad_maximum_fusion
  190.5 74.7 %all-gather.2.cloned.1.call-done = bf16[512,2,2,2560]{3,2,1,0:T(2,128)(2,1)} async-done(((bf16[8,2,2,2560]{3,2,1,0:T(2,128)(2,1)}), bf16[512,2,2,2560]{3,2,1,0:T(2,128)(2,1)}) %all-gather.2.cloned.1.call-update) | async-done | bytes 10485776 | tf_op jit(solution)/shard_map/all_gather | solution.py:64
  265.2 13.0 %reshape.97 = bf16[64,81920]{1,0:T(8,128)(2,1)} reshape(bf16[512,2,2,2560]{3,2,1,0:T(2,128)(2,1)} %all-gather.2.cloned.1.call-done) | data formatting | bytes 20971520 | tf_op jit(solution)/shard_map/reshape | solution.py:65
  278.2 13.8 %dot_general.11 = bf16[8,2,2,2560,64]{3,2,1,0,4:T(2,128)(2,1)} reshape(bf16[81920,64]{0,1:T(8,128)(2,1)} %bitcast.71) | data formatting | bytes 20971520 | tf_op jit(solution)/shard_map/dot_general | solution.py:66
  292.0 16.1 %fusion.8 = f32[4,8,2,2,2560]{4,0,3,2,1:T(4,128)} fusion(bf16[8,2,2,2560,64]{3,2,1,0,4:T(2,128)(2,1)} %dot_general.11, s32[64]{0:T(128)S(1)} %add_reduce_fusion, pred[64]{0:T(512)(128)(4,1)S(1)} %fusion.14), kind=kOutput, calls=%fused_computation.19 | convolution fusion | flops 41943552 | bytes 11796800 | tf_op jit(solution)/shard_map/dot_general | solution.py:66
  308.2 51.6 %while.10 = (s32[]{:T(128)}, f32[4,8,128,256]{3,2,1,0:T(8,128)}, f32[4,8,2,2,2560]{4,0,3,2,1:T(4,128)}, bf16[2,128,2560]{2,1,0:T(8,128)(2,1)S(1)}, bf16[2,128,25...) while((s32[]{:T(128)}, f32[4,8,128,256]{3,2,1,0:T(8,128)}, ...), condition=%wide.region_4.5_spmd, body=%wide.region_3.4_spmd.sunk | while | flops 2748841984 | bytes 53281388 | solution.py:89
  308.5 1.7 constant_dynamic-slice_fusion.3
  310.2 0.2 copy.51
  310.3 0.2 fusion.28
  310.6 0.7 bitcast_convert_fusion.5
  311.3 0.0 copy-start.2
  311.3 5.8 %add_convert_fusion.2 = (bf16[8,128,2560]{2,1,0:T(8,128)(2,1)S(1)}, bf16[8,128,2560]{2,1,0:T(8,128)(2,1)S(1)}) fusion(f32[128,2560]{1,0:T(8,128)S(1)} %get-tuple-element.145, f32[8,2560]{1,0:T(8,128)S(1)} %get-tuple-element.148, f32[128,2560]{1,0:T(8,128)S(1)} %get-tuple-element.149, f32[8,2560]{1,0:T(8,128)S(1)} %get-tuple-element.150, ...), kind=kLoop, calls=%fused_computation.5.clone.1 | loop fusion | flops 41943040 | bytes 16056320 | tf_op jit(solution)/shard_map/convert.7
  317.1 0.0 copy-done.2
  317.1 3.1 fusion.29
  320.2 1.1 constant_dynamic-update-slice_fusion.2
  321.3 1.7 constant_dynamic-slice_fusion.3
  323.0 0.2 copy.51
  323.1 0.2 fusion.28
  323.4 0.7 bitcast_convert_fusion.5
  324.1 5.8 %add_convert_fusion.2 = (bf16[8,128,2560]{2,1,0:T(8,128)(2,1)S(1)}, bf16[8,128,2560]{2,1,0:T(8,128)(2,1)S(1)}) fusion(f32[128,2560]{1,0:T(8,128)S(1)} %get-tuple-element.145, f32[8,2560]{1,0:T(8,128)S(1)} %get-tuple-element.148, f32[128,2560]{1,0:T(8,128)S(1)} %get-tuple-element.149, f32[8,2560]{1,0:T(8,128)S(1)} %get-tuple-element.150, ...), kind=kLoop, calls=%fused_computation.5.clone.1 | loop fusion | flops 41943040 | bytes 16056320 | tf_op jit(solution)/shard_map/convert.7
  329.9 3.1 fusion.29
  333.0 1.1 constant_dynamic-update-slice_fusion.2
  334.1 1.7 constant_dynamic-slice_fusion.3
  335.8 0.2 copy.51
  336.0 0.2 fusion.28
  336.2 0.7 bitcast_convert_fusion.5
  336.9 0.0 copy-start.2
  336.9 5.8 %add_convert_fusion.2 = (bf16[8,128,2560]{2,1,0:T(8,128)(2,1)S(1)}, bf16[8,128,2560]{2,1,0:T(8,128)(2,1)S(1)}) fusion(f32[128,2560]{1,0:T(8,128)S(1)} %get-tuple-element.145, f32[8,2560]{1,0:T(8,128)S(1)} %get-tuple-element.148, f32[128,2560]{1,0:T(8,128)S(1)} %get-tuple-element.149, f32[8,2560]{1,0:T(8,128)S(1)} %get-tuple-element.150, ...), kind=kLoop, calls=%fused_computation.5.clone.1 | loop fusion | flops 41943040 | bytes 16056320 | tf_op jit(solution)/shard_map/convert.7
  342.7 3.1 fusion.29
  345.8 1.1 constant_dynamic-update-slice_fusion.2
  346.9 1.7 constant_dynamic-slice_fusion.3
  348.6 0.2 copy.51
  348.8 0.2 fusion.28
  349.1 0.7 bitcast_convert_fusion.5
  349.8 5.8 %add_convert_fusion.2 = (bf16[8,128,2560]{2,1,0:T(8,128)(2,1)S(1)}, bf16[8,128,2560]{2,1,0:T(8,128)(2,1)S(1)}) fusion(f32[128,2560]{1,0:T(8,128)S(1)} %get-tuple-element.145, f32[8,2560]{1,0:T(8,128)S(1)} %get-tuple-element.148, f32[128,2560]{1,0:T(8,128)S(1)} %get-tuple-element.149, f32[8,2560]{1,0:T(8,128)S(1)} %get-tuple-element.150, ...), kind=kLoop, calls=%fused_computation.5.clone.1 | loop fusion | flops 41943040 | bytes 16056320 | tf_op jit(solution)/shard_map/convert.7
  355.6 3.1 fusion.29
  358.6 1.1 constant_dynamic-update-slice_fusion.2
  359.7 0.0 all-reduce.2.cloned.1.call-update
  359.8 94.6 %all-reduce.2.cloned.1.call-done = f32[4,8,128,256]{3,2,1,0:T(8,128)} async-done(((f32[4,8,128,256]{3,2,1,0:T(8,128)}), f32[4,8,128,256]{3,2,1,0:T(8,128)}) %all-reduce.2.cloned.1.call-update) | async-done | bytes 4194320 | tf_op jit(solution)/shard_map/psum | solution.py:90
  454.4 2.3 constant_dynamic-slice_fusion.1
  (20 shorter events, 0.2 us)
Async XLA Ops:
  6.5 258.7 %all-gather.2.cloned.1.call-start = ((), (), s32[]{:S(2)}) async-start(), calls=%async_computation | async-start | bytes 10649600 | tf_op jit(solution)/shard_map/all_gather | solution.py:64
  10.1 2.3 copy-start
  146.4 20.6 %copy-start.1 = (bf16[2,128,2560]{1,2,0:T(8,128)(2,1)}, bf16[2,128,2560]{1,2,0:T(8,128)(2,1)S(1)}, u32[]{:S(2)}) copy-start(bf16[2,128,2560]{1,2,0:T(8,128)(2,1)S(1)} %get-tuple-element.91) | copy-start | bytes 3932164
  174.4 280.0 %all-reduce.2.cloned.1.call-start = ((), (), s32[]{:S(2)}) async-start(), calls=%async_computation.1 | async-start | bytes 8388608 | tf_op jit(solution)/shard_map/psum | solution.py:90
  174.4 2.3 copy-start.3
  174.4 2.3 copy-start.4
  311.3 5.8 %copy-start.2 = (bf16[5120,256]{1,0:T(8,128)(2,1)S(1)}, bf16[5120,256]{1,0:T(8,128)(2,1)}, u32[]{:S(2)}) copy-start(bf16[5120,256]{1,0:T(8,128)(2,1)} %get-tuple-element.178) | copy-start | bytes 7864324 | tf_op jit(solution)/shard_map/while
  324.1 5.8 %copy-start.2 = (bf16[5120,256]{1,0:T(8,128)(2,1)S(1)}, bf16[5120,256]{1,0:T(8,128)(2,1)}, u32[]{:S(2)}) copy-start(bf16[5120,256]{1,0:T(8,128)(2,1)} %get-tuple-element.178) | copy-start | bytes 7864324 | tf_op jit(solution)/shard_map/while
  336.9 5.8 %copy-start.2 = (bf16[5120,256]{1,0:T(8,128)(2,1)S(1)}, bf16[5120,256]{1,0:T(8,128)(2,1)}, u32[]{:S(2)}) copy-start(bf16[5120,256]{1,0:T(8,128)(2,1)} %get-tuple-element.178) | copy-start | bytes 7864324 | tf_op jit(solution)/shard_map/while
  349.7 5.8 %copy-start.2 = (bf16[5120,256]{1,0:T(8,128)(2,1)S(1)}, bf16[5120,256]{1,0:T(8,128)(2,1)}, u32[]{:S(2)}) copy-start(bf16[5120,256]{1,0:T(8,128)(2,1)} %get-tuple-element.178) | copy-start | bytes 7864324 | tf_op jit(solution)/shard_map/while
Sparse Core Ops, SparseCore 0:
  174.5 90.6 all-gather.1
  359.9 94.4 all-reduce.1
where the time goes:
time: 467 us; the launch traced here: 464 us
  other arithmetic  178 us (38%)
  waiting for transfers between devices  169 us (36%)
  local copies, waits for them, and re-layouts  73.9 us (16%)
  matrix products  28.4 us (6%)
  between operations  14.1 us (3%)
    another operation x1, other arithmetic, whiten(): lax.reduce_window(amplitude, jnp.zeros((), amplitude.dtype), lax.add, win...  129 us
    psum x1, waiting for transfers between devices, shards(): summed_hours = lax.psum(partial_stacks, 'hour')  94.6 us
    all_gather x1, waiting for transfers between devices, shards(): gathered = lax.all_gather(local_sources, 'chan', axis=0, tiled=True)  74.7 us
    another operation x6, other arithmetic  34.9 us
    dot_general x1, matrix products, shards(): chosen = jnp.dot(onehot, flattened, preferred_element_type=jnp.float32)  16.1 us
    dot_general x1, local copies, waits for them, and re-layouts, shards(): chosen = jnp.dot(onehot, flattened, preferred_element_type=jnp.float32)  13.8 us
    reshape x1, local copies, waits for them, and re-layouts, shards(): flattened = gathered.reshape(block_count, -1)  13 us
    dot_general x4, matrix products, one_slot(): jnp.dot(cross, table_values, preferred_element_type=jnp.float32)  12.3 us
  transfers between devices with their start and end apart: 2, of which 2 were waited for; matrix products, arithmetic and copies ran while one was open for 3% of the time, Pallas kernels for 0%

commit v1 on v0

v1 whole, which is shorter than its diff:
```python
import functools
import math

import jax
import jax.numpy as jnp
import ml_dtypes
import numpy as np
from jax import lax
from jax.experimental import pallas as pl
from jax.experimental.pallas import tpu as pltpu
from jax.sharding import PartitionSpec as P

VS = 8
CH = 128
F = 2560
F0 = 64
NWIN = 8192
SMOOTH = 129
LAGS = 256
WIN = 2
QUARTERS = 4
FQ = F // QUARTERS
GROUP = 4


def lag_table():
    bins = np.arange(F, dtype=np.int64)[:, None] + F0
    lags = np.arange(LAGS, dtype=np.int64)[None, :] - LAGS // 2
    phase = bins * (lags % NWIN) % NWIN
    angle = phase.astype(np.float32) * np.float32(2.0 * math.pi / NWIN)
    real = np.cos(angle).reshape(QUARTERS, FQ, LAGS)
    imag = -np.sin(angle).reshape(QUARTERS, FQ, LAGS)
    return np.concatenate([real, imag], 1).astype(ml_dtypes.bfloat16)


def band_matrix():
    bin_in = lax.broadcasted_iota(jnp.int32, (512, 256), 0) - 128
    bin_out = lax.broadcasted_iota(jnp.int32, (512, 256), 1)
    half = SMOOTH // 2
    inside = (bin_in - bin_out <= half) & (bin_out - bin_in <= half)
    return jnp.where(inside, 1.0, 0.0).astype(jnp.bfloat16)


def inverse_mean(real, imag, band):
    amplitude = jnp.sqrt(real * real + imag * imag)
    high = amplitude.astype(jnp.bfloat16)
    low = (amplitude - high.astype(jnp.float32)).astype(jnp.bfloat16)
    zeros = jnp.zeros((amplitude.shape[0], 128), jnp.bfloat16)
    high = jnp.concatenate([zeros, high, zeros], 1)
    low = jnp.concatenate([zeros, low, zeros], 1)
    parts = []
    for start in range(0, F, 256):
        total = jnp.dot(high[:, start:start + 512], band, preferred_element_type=jnp.float32)
        total += jnp.dot(low[:, start:start + 512], band, preferred_element_type=jnp.float32)
        parts.append(1.0 / (total / SMOOTH + 1e-06))
    return jnp.concatenate(parts, 1)


def whiten_kernel(x_ref, white_ref, source_ref):
    band = band_matrix()
    row = lax.broadcasted_iota(jnp.int32, (VS, CH), 0)
    col = lax.broadcasted_iota(jnp.int32, (VS, CH), 1)
    pick = jnp.where(col == row * (CH // VS), 1.0, 0.0).astype(jnp.bfloat16)
    for w in range(WIN):
        for c in range(0, CH, 64):
            real = x_ref[w, 0, c:c + 64, :].astype(jnp.float32)
            imag = x_ref[w, 1, c:c + 64, :].astype(jnp.float32)
            inverse = inverse_mean(real, imag, band)
            white_ref[w, 0, c:c + 64, :] = (real * inverse).astype(jnp.bfloat16)
            white_ref[w, 1, c:c + 64, :] = (imag * inverse).astype(jnp.bfloat16)
        for p in range(2):
            rows = jnp.dot(pick, white_ref[w, p], preferred_element_type=jnp.float32)
            for v in range(VS):
                source_ref[v * WIN + w, p:p + 1, :] = rows[v:v + 1].astype(jnp.bfloat16)


def whiten(x):
    return pl.pallas_call(
        whiten_kernel,
        out_shape=(
            jax.ShapeDtypeStruct((WIN, 2, CH, F), jnp.bfloat16),
            jax.ShapeDtypeStruct((VS * WIN, 2, F), jnp.bfloat16),
        ),
        in_specs=[pl.BlockSpec(memory_space=pltpu.VMEM)],
        out_specs=[pl.BlockSpec(memory_space=pltpu.VMEM)] * 2,
        compiler_params=pltpu.CompilerParams(vmem_limit_bytes=50 << 20),
    )(x)


def stack_kernel(scale, source_ref, white_ref, table_ref, out_ref, total_ref):
    def one_slot(slot, carry):
        for q in range(QUARTERS):
            bins = slice(q * FQ, (q + 1) * FQ)
            for first in range(0, VS, GROUP):
                rows = []
                for v in range(first, first + GROUP):
                    xr = [white_ref[w, 0, :, bins].reshape(8, 16, FQ) for w in range(WIN)]
                    xi = [white_ref[w, 1, :, bins].reshape(8, 16, FQ) for w in range(WIN)]
                    s = []
                    for w in range(WIN):
                        both = source_ref[(v * WIN + w) * QUARTERS + q, slot].astype(jnp.float32)
                        for p in range(2):
                            one = jnp.broadcast_to(both[p:p + 1], (16, FQ))
                            s.append(one.astype(jnp.bfloat16)[None])
                    real = (s[0] * xr[0] + s[1] * xi[0]) + (s[2] * xr[1] + s[3] * xi[1])
                    imag = (s[1] * xr[0] - s[0] * xi[0]) + (s[3] * xr[1] - s[2] * xi[1])
                    rows.append(jnp.concatenate([real.reshape(CH, FQ), imag.reshape(CH, FQ)], 1))
                lagged = jnp.dot(
                    jnp.concatenate(rows, 0), table_ref[q], preferred_element_type=jnp.float32
                )
                out = slice(first * CH, (first + GROUP) * CH)
                if q == 0:
                    total_ref[out] = lagged
                elif q < QUARTERS - 1:
                    total_ref[out] += lagged
                else:
                    out_ref[slot, out] = ((total_ref[out] + lagged) * scale).astype(jnp.bfloat16)
        return carry

    lax.fori_loop(0, out_ref.shape[0], one_slot, 0)


def stack(source, white, table, scale):
    slots = source.shape[1]
    return pl.pallas_call(
        functools.partial(stack_kernel, scale),
        out_shape=jax.ShapeDtypeStruct((slots, VS * CH, LAGS), jnp.bfloat16),
        in_specs=[pl.BlockSpec(memory_space=pltpu.VMEM)] * 3,
        out_specs=pl.BlockSpec(memory_space=pltpu.VMEM),
        scratch_shapes=[pltpu.VMEM((VS * CH, LAGS), jnp.float32)],
        compiler_params=pltpu.CompilerParams(vmem_limit_bytes=50 << 20),
    )(source, white, table)


def slot_sources(partner_lists, partner_counts):
    blocks, most = partner_lists.shape
    offsets = jnp.arange(most, dtype=jnp.int32)
    live = offsets[None, :] < partner_counts[:, None]
    receivers = jnp.arange(blocks, dtype=jnp.int32)
    member = jnp.any((partner_lists[None] == receivers[:, None, None]) & live[None], 2)
    below = receivers[:, None] < receivers[None, :]
    rank = jnp.sum(member[:, :, None] & below[None], 1, dtype=jnp.int32)
    hit = member[:, None, :] & (rank[:, None, :] == offsets[None, :, None])
    source = jnp.sum(jnp.where(hit, receivers[None, None, :], 0), 2, dtype=jnp.int32)
    return jnp.where(jnp.any(hit, 2), source, blocks)


def shards(spectra, partner_lists, partner_counts):
    blocks = partner_lists.shape[0]
    slots = partner_lists.shape[1]
    hours = lax.axis_size("hour")
    scale = 1.0 / math.sqrt(4.0 * F * WIN * hours)
    white, source = whiten(spectra)
    chunks = source.reshape(VS * WIN, 2, QUARTERS, FQ).transpose(0, 2, 1, 3)
    chunks = chunks.reshape(blocks, 2 * FQ)
    mine = lax.all_to_all(chunks, "chan", 0, 0, tiled=True)
    mine = jnp.concatenate([mine, jnp.zeros((1, 2 * FQ), jnp.bfloat16)], 0)
    wanted = slot_sources(partner_lists, partner_counts)
    chosen = mine[wanted.reshape(-1)].reshape(blocks, slots * 2 * FQ)
    arrived = lax.all_to_all(chosen, "chan", 0, 0, tiled=True)
    arrived = arrived.reshape(blocks, slots, 2, FQ)
    partial = stack(arrived, white, jnp.asarray(lag_table()), scale)
    hourly = lax.all_to_all(partial, "hour", 0, 0, tiled=True)
    total = jnp.sum(hourly.astype(jnp.float32), 0)
    return total.reshape(1, VS, CH, LAGS)


def solution(mesh):
    return jax.shard_map(
        shards,
        mesh=mesh,
        in_specs=(P("hour", None, "chan", None), P(), P()),
        out_specs=P(("chan", "hour"), None, None, None),
        check_vma=False,
    )
```

time: 467 us -> 117 us (0.25)
  other arithmetic: 178 us -> 12.5 us
  waiting for transfers between devices: 169 us -> 9.18 us
  local copies, waits for them, and re-layouts: 73.9 us -> 6.28 us
  blocking collectives: 0 us -> 55 us
  matrix products: 28.4 us -> 0 us
  Pallas kernels: 0 us -> 20.3 us
  between operations: 14.1 us -> 0.18 us
  starting transfers between devices: 0.04 us -> 13.2 us
    another operation x7 -> x0, other arithmetic: 164 us -> none  [the longest x1 129 us: whiten(): lax.reduce_window(amplitude, jnp.zeros((), amplitude.dtype), lax.add, win...]
    psum x1 -> x0, waiting for transfers between devices: 94.6 us -> none  [shards(): summed_hours = lax.psum(partial_stacks, 'hour')]
    all_gather x1 -> x0, waiting for transfers between devices: 74.7 us -> none  [shards(): gathered = lax.all_gather(local_sources, 'chan', axis=0, tiled=True)]
    all_to_all x0 -> x2, blocking collectives: none -> 55 us  [the longest x1 29.7 us: shards(): hourly = lax.all_to_all(partial, 'hour', 0, 0, tiled=True)]
    dot_general x5 -> x0, matrix products: 28.4 us -> none  [the longest x1 16.1 us: shards(): chosen = jnp.dot(onehot, flattened, preferred_element_type=jnp.float32)]
    slice x6 -> x0, local copies, waits for them, and re-layouts: 21.6 us -> none  [the longest x1 10.4 us: shards(): white_re[:, ::stride, :]]
    pallas_call x0 -> x2, Pallas kernels: none -> 20.3 us  [the longest x1 15.1 us: stack(): pl.pallas_call(functools.partial(stack_kernel, scale), out_shape=jax.Shap...]
    dot_general x1 -> x0, local copies, waits for them, and re-layouts: 13.8 us -> none  [shards(): chosen = jnp.dot(onehot, flattened, preferred_element_type=jnp.float32)]
  transfers between devices with their start and end apart: 2 -> 1, of which waited for: 2 -> 1; matrix products, arithmetic and copies ran while one was open for 3% -> 1% of each run, Pallas kernels for 0% -> 0%
where the time goes in v1:
time: 117 us
  blocking collectives  55 us (47%)
  Pallas kernels  20.3 us (17%)
  starting transfers between devices  13.2 us (11%)
  other arithmetic  12.5 us (11%)
  waiting for transfers between devices  9.18 us (8%)
  local copies, waits for them, and re-layouts  6.28 us (5%)
    all_to_all x1, blocking collectives, shards(): hourly = lax.all_to_all(partial, 'hour', 0, 0, tiled=True)  29.7 us
    all_to_all x1, blocking collectives, shards(): arrived = lax.all_to_all(chosen, 'chan', 0, 0, tiled=True)  25.3 us
    pallas_call x1, Pallas kernels, stack(): pl.pallas_call(functools.partial(stack_kernel, scale), out_shape=jax.Shap...  15.1 us
    all_to_all x1, starting transfers between devices, shards(): mine = lax.all_to_all(chunks, 'chan', 0, 0, tiled=True)  13.2 us
    all_to_all x1, waiting for transfers between devices, shards(): mine = lax.all_to_all(chunks, 'chan', 0, 0, tiled=True)  9.18 us
    all_to_all x2, other arithmetic, shards(): arrived = lax.all_to_all(chosen, 'chan', 0, 0, tiled=True)  8.47 us
    pallas_call x1, Pallas kernels, whiten(): pl.pallas_call(whiten_kernel, out_shape=(jax.ShapeDtypeStruct((WIN, 2, CH...  5.22 us
    unnamed x11, local copies, waits for them, and re-layouts  3.37 us
  transfers between devices with their start and end apart: 1, of which 1 were waited for; matrix products, arithmetic and copies ran while one was open for 1% of the time, Pallas kernels for 0%

profile of v1, /device:TPU:1, one launch (start us, length us, event | category | flops | bytes accessed | tf_op | source)
XLA Modules:
  0.0 116.5 jit_solution(770919586602011775)
XLA Ops:
  0.0 0.0 copy-start.2
  0.0 0.0 copy-start.1
  0.0 5.2 %shard_map.46 = (bf16[2,2,128,2560]{3,2,1,0:T(8,128)(2,1)S(1)}, bf16[16,2,2560]{2,1,0:T(2,128)(2,1)S(1)}) custom-call(bf16[2,2,128,2560]{3,2,1,0:T(8,128)(2,1)} %x_ref.1), custom_call_target="tpu_custom_call" | custom-call | tf_op jit(solution)/shard_map/pallas_call | solution.py:78
  5.2 0.0 copy-start
  5.2 1.5 %copy-done = bf16[2,2,128,2560]{3,2,1,0:T(8,128)(2,1)} copy-done((bf16[2,2,128,2560]{3,2,1,0:T(8,128)(2,1)}, bf16[2,2,128,2560]{3,2,1,0:T(8,128)(2,1)S(1)}, u32[]{:S(2)}) %copy-start) | copy-done | bytes 2621464
  6.7 0.1 all_to_all.23
  6.9 0.5 broadcast.50
  7.4 1.6 %reduce.1 = bf16[64,1280]{1,0:T(8,128)(2,1)S(1)} reduce(bf16[64,1,1280]{2,1,0:T(2,128)(2,1)S(1)} %all_to_all.23, bf16[]{:T(256)} %broadcast.50), dimensions={1}, to_apply=%all_to_all.23.reduce_sub_computation | reduce | bytes 327682 | tf_op jit(solution)/shard_map/all_to_all | solution.py:156
  9.0 0.7 reshape.95
  9.7 13.2 %all-to-all-start = ((bf16[64,2,640]{2,1,0:T(2,128)(2,1)}), bf16[64,2,640]{2,1,0:T(2,128)(2,1)S(1)}, u32[]{:S(2)}, u32[]{:S(2)}) async-start(bf16[64,2,640]{2,1,0:T(2,128)(2,1)} %reshape.95), calls=%async_computation | async-start | bytes 327680 | tf_op jit(solution)/shard_map/all_to_all | solution.py:156
  22.8 0.0 copy-done.2
  22.9 0.0 copy-done.1
  22.9 0.8 convert_reduce_fusion.1
  23.7 0.1 fusion.3
  23.8 0.2 select_reduce_fusion
  24.0 0.1 copy.18
  24.1 0.1 select_n.31
  24.2 9.2 %all-to-all-done = bf16[64,2,640]{2,1,0:T(2,128)(2,1)S(1)} async-done(((bf16[64,2,640]{2,1,0:T(2,128)(2,1)}), bf16[64,2,640]{2,1,0:T(2,128)(2,1)S(1)}, u32[]{:S(2)}, u32[]{:S(2)}) %all-to-all-start) | async-done | bytes 163872 | tf_op jit(solution)/shard_map/all_to_all | solution.py:156
  33.4 0.1 reshape.96
  33.6 1.2 %gather_fusion = bf16[256,1280]{1,0:T(8,128)(2,1)S(1)} fusion(bf16[65,1280]{1,0:T(8,128)(2,1)S(1)} %concatenate.3, s32[1024]{0:T(1024)S(1)} %pad_clamp_fusion), kind=kCustom, calls=%fused_computation | custom fusion | bytes 1311744 | tf_op jit(solution)/shard_map/gather | solution.py:159
  34.8 0.3 all_to_all.24
  35.2 4.5 %reduce.2 = bf16[64,5120]{1,0:T(8,128)(2,1)S(1)} reduce(bf16[64,1,5120]{2,1,0:T(2,128)(2,1)S(1)} %all_to_all.24, bf16[]{:T(256)} %broadcast.50), dimensions={1}, to_apply=%all_to_all.24.reduce_sub_computation | reduce | bytes 1310722 | tf_op jit(solution)/shard_map/all_to_all | solution.py:160
  39.7 0.5 reshape.97
  40.2 25.3 %all_to_all.28 = bf16[64,2,2560]{2,1,0:T(2,128)(2,1)S(1)} all-to-all(bf16[64,2,2560]{2,1,0:T(2,128)(2,1)S(1)} %reshape.97), channel_id=1, replica_groups=mesh['chan'=64,'hour'=4] {'chan'}, dimensions={0} | all-to-all | bytes 1310720 | tf_op jit(solution)/shard_map/all_to_all | solution.py:160
  65.5 0.5 reshape.98
  66.0 3.9 %reduce = bf16[64,5120]{1,0:T(8,128)(2,1)S(1)} reduce(bf16[64,1,5120]{2,1,0:T(2,128)(2,1)S(1)} %reshape.98, bf16[]{:T(256)} %constant.19), dimensions={1}, to_apply=%all_to_all.21.reduce_sub_computation | reduce | bytes 1310722 | tf_op jit(solution)/shard_map/all_to_all | solution.py:160
  69.9 0.5 reshape.84.source_ref
  70.4 15.1 %shard_map.47 = bf16[4,1024,256]{2,1,0:T(8,128)(2,1)S(1)} custom-call(bf16[64,4,2,640]{3,2,1,0:T(2,128)(2,1)S(1)} %reshape.84.source_ref, bf16[2,2,128,2560]{3,2,1,0:T(8,128)(2,1)} %copy-done, bf16[4,1280,256]{2,1,0:T(8,128)(2,1)} %constant.6.clone.table_ref), custom_call_target="tpu_custom_call" | custom-call | tf_op jit(solution)/shard_map/pallas_call | solution.py:125
  85.5 29.7 %all_to_all.29 = bf16[4,1024,256]{2,1,0:T(8,128)(2,1)S(1)} all-to-all(bf16[4,1024,256]{2,1,0:T(8,128)(2,1)S(1)} %shard_map.47), channel_id=1, replica_groups=mesh['chan'=64,'hour'=4] {'hour'}, dimensions={0} | all-to-all | bytes 4194304 | tf_op jit(solution)/shard_map/all_to_all | solution.py:163
  115.2 1.3 %convert_reduce_fusion = f32[1024,256]{1,0:T(8,128)} fusion(bf16[4,1024,256]{2,1,0:T(8,128)(2,1)S(1)} %all_to_all.29), kind=kLoop, calls=%fused_computation.1 | loop fusion | flops 1835008 | bytes 3145728 | tf_op jit(solution)/shard_map/reduce_sum | solution.py:164
  (8 shorter events, 0.1 us)
Async XLA Ops:
  0.0 22.9 %copy-start.2 = (s32[64]{0:T(128)S(1)}, s32[64]{0:T(128)}, u32[]{:S(2)}) copy-start(s32[64]{0:T(128)} %param.6) | copy-start | bytes 772
  0.0 22.9 %copy-start.1 = (s32[64,4]{0,1:T(4,128)S(1)}, s32[64,4]{0,1:T(4,128)}, u32[]{:S(2)}) copy-start(s32[64,4]{0,1:T(4,128)} %param.5) | copy-start | bytes 3076
  5.2 1.5 %copy-start = (bf16[2,2,128,2560]{3,2,1,0:T(8,128)(2,1)}, bf16[2,2,128,2560]{3,2,1,0:T(8,128)(2,1)S(1)}, u32[]{:S(2)}) copy-start(bf16[2,2,128,2560]{3,2,1,0:T(8,128)(2,1)S(1)} %get-tuple-element.8.white_ref) | copy-start | bytes 7864324
  9.7 23.8 %all-to-all-start = ((bf16[64,2,640]{2,1,0:T(2,128)(2,1)}), bf16[64,2,640]{2,1,0:T(2,128)(2,1)S(1)}, u32[]{:S(2)}, u32[]{:S(2)}) async-start(bf16[64,2,640]{2,1,0:T(2,128)(2,1)} %reshape.95), calls=%async_computation | async-start | bytes 327680 | tf_op jit(solution)/shard_map/all_to_all | solution.py:156

commit v2 on v1

v2 whole, which is shorter than its diff:
```python
import functools
import math

import jax
import jax.numpy as jnp
import ml_dtypes
import numpy as np
from jax import lax
from jax.experimental import pallas as pl
from jax.experimental.pallas import tpu as pltpu
from jax.sharding import PartitionSpec as P

VS = 8
CH = 128
F = 2560
F0 = 64
NWIN = 8192
SMOOTH = 129
LAGS = 256
WIN = 2
QUARTERS = 4
FQ = F // QUARTERS
GROUP = 4


def lag_table():
    bins = np.arange(F, dtype=np.int64)[:, None] + F0
    lags = np.arange(LAGS, dtype=np.int64)[None, :] - LAGS // 2
    phase = bins * (lags % NWIN) % NWIN
    angle = phase.astype(np.float32) * np.float32(2.0 * math.pi / NWIN)
    real = np.cos(angle).reshape(QUARTERS, FQ, LAGS)
    imag = -np.sin(angle).reshape(QUARTERS, FQ, LAGS)
    return np.concatenate([real, imag], 1).astype(ml_dtypes.bfloat16)


def band_matrix():
    bin_in = lax.broadcasted_iota(jnp.int32, (512, 256), 0) - 128
    bin_out = lax.broadcasted_iota(jnp.int32, (512, 256), 1)
    half = SMOOTH // 2
    inside = (bin_in - bin_out <= half) & (bin_out - bin_in <= half)
    return jnp.where(inside, 1.0, 0.0).astype(jnp.bfloat16)


def inverse_mean(real, imag, band):
    amplitude = jnp.sqrt(real * real + imag * imag)
    high = amplitude.astype(jnp.bfloat16)
    low = (amplitude - high.astype(jnp.float32)).astype(jnp.bfloat16)
    zeros = jnp.zeros((amplitude.shape[0], 128), jnp.bfloat16)
    high = jnp.concatenate([zeros, high, zeros], 1)
    low = jnp.concatenate([zeros, low, zeros], 1)
    parts = []
    for start in range(0, F, 256):
        total = jnp.dot(high[:, start:start + 512], band, preferred_element_type=jnp.float32)
        total += jnp.dot(low[:, start:start + 512], band, preferred_element_type=jnp.float32)
        parts.append(1.0 / (total / SMOOTH + 1e-06))
    return jnp.concatenate(parts, 1)


def pick_matrix():
    row = lax.broadcasted_iota(jnp.int32, (VS, CH), 0)
    col = lax.broadcasted_iota(jnp.int32, (VS, CH), 1)
    return jnp.where(col == row * (CH // VS), 1.0, 0.0).astype(jnp.bfloat16)


def whiten_window(x_ref, white_ref, band, w):
    for c in range(0, CH, 64):
        real = x_ref[w, 0, c:c + 64, :].astype(jnp.float32)
        imag = x_ref[w, 1, c:c + 64, :].astype(jnp.float32)
        inverse = inverse_mean(real, imag, band)
        white_ref[w, 0, c:c + 64, :] = (real * inverse).astype(jnp.bfloat16)
        white_ref[w, 1, c:c + 64, :] = (imag * inverse).astype(jnp.bfloat16)


def whiten_sources(x_ref, chunk_ref, band):
    pick = pick_matrix()
    parts = []
    for p in range(2):
        rows = [jnp.dot(pick, x_ref[w, p], preferred_element_type=jnp.float32) for w in range(WIN)]
        parts.append(jnp.concatenate(rows, 0))
    inverse = inverse_mean(parts[0], parts[1], band)
    for p in range(2):
        white = parts[p] * inverse
        for w in range(WIN):
            for v in range(VS):
                row = w * VS + v
                for q in range(QUARTERS):
                    one = white[row:row + 1, q * FQ:(q + 1) * FQ].astype(jnp.bfloat16)
                    chunk_ref[(v * WIN + w) * QUARTERS + q, p:p + 1, :] = one


def half_stack(source_ref, white_ref, table_ref, total_ref, order, first):
    for q in range(QUARTERS):
        bins = slice(q * FQ, (q + 1) * FQ)
        xr = [white_ref[w, 0, :, bins].reshape(8, 16, FQ) for w in range(WIN)]
        xi = [white_ref[w, 1, :, bins].reshape(8, 16, FQ) for w in range(WIN)]
        rows = []
        for v in range(GROUP):
            s = []
            for w in range(WIN):
                chunk = ((first + v) * WIN + w) * QUARTERS + q
                both = source_ref[order, chunk].astype(jnp.float32)
                for p in range(2):
                    one = jnp.broadcast_to(both[p:p + 1], (16, FQ))
                    s.append(one.astype(jnp.bfloat16)[None])
            real = (s[0] * xr[0] + s[1] * xi[0]) + (s[2] * xr[1] + s[3] * xi[1])
            imag = (s[1] * xr[0] - s[0] * xi[0]) + (s[3] * xr[1] - s[2] * xi[1])
            rows.append(jnp.concatenate([real.reshape(CH, FQ), imag.reshape(CH, FQ)], 1))
        lagged = jnp.dot(
            jnp.concatenate(rows, 0), table_ref[q], preferred_element_type=jnp.float32
        )
        if q == 0:
            total_ref[...] = lagged
        else:
            total_ref[...] += lagged


def fused_kernel(
    scale, blocks, hours, wanted_ref, x_ref, table_ref, out_ref,
    white_ref, chunk_ref, mine_ref, chosen_ref, source_ref, total_ref,
    far_out, far_in, near_out, near_in,
    spread_out, spread_in, slot_out, slot_in, far_out_sem, far_in_sem, near_out_sem, near_in_sem,
):
    me = lax.axis_index("chan")
    hour = lax.axis_index("hour")
    above = lax.rem(hour + 1, hours)
    below = lax.rem(hour + hours - 1, hours)
    barrier = pltpu.get_barrier_semaphore()

    def greet(k, carry):
        pl.semaphore_signal(barrier, inc=1, device_id={"chan": lax.rem(me + k, blocks)})
        return carry

    lax.fori_loop(1, blocks, greet, 0)
    for to in (above, below):
        pl.semaphore_signal(barrier, inc=1, device_id={"hour": to})

    band = band_matrix()
    whiten_sources(x_ref, chunk_ref, band)
    mine_ref[blocks] = jnp.zeros(mine_ref.shape[1:], jnp.bfloat16)
    mine_ref[me] = chunk_ref[me]
    pl.semaphore_wait(barrier, blocks + 1)

    def spread(k, carry):
        to = lax.rem(me + k, blocks)
        pltpu.make_async_remote_copy(
            chunk_ref.at[to], mine_ref.at[me], spread_out, spread_in, device_id={"chan": to}
        ).start()
        return carry

    lax.fori_loop(1, blocks, spread, 0)
    whiten_window(x_ref, white_ref, band, 0)
    others = mine_ref.at[pl.ds(0, blocks - 1)]
    pltpu.make_async_copy(others, others, spread_in).wait()

    def slot_of(order):
        return lax.rem(hour + jnp.where(order == 0, 2, jnp.where(order == 3, 0, 2 * order - 1)), hours)

    def choose(order, carry):
        slot = slot_of(order)

        def one(k, inner):
            to = lax.rem(me + k, blocks)
            chosen_ref[order, to] = mine_ref[wanted_ref[to, slot]]
            pltpu.make_async_remote_copy(
                chosen_ref.at[order, to], source_ref.at[order, me],
                slot_out.at[order], slot_in.at[order], device_id={"chan": to},
            ).start()
            return inner

        lax.fori_loop(1, blocks, one, 0)
        source_ref[order, me] = mine_ref[wanted_ref[me, slot]]
        return carry

    lax.fori_loop(0, hours, choose, 0)
    whiten_window(x_ref, white_ref, band, 1)

    def arrive(order):
        part = source_ref.at[order, pl.ds(0, blocks - 1)]
        pltpu.make_async_copy(part, part, slot_in.at[order]).wait()

    def far_copy(side, to):
        return pltpu.make_async_remote_copy(
            far_out.at[side], far_in.at[side], far_out_sem.at[side], far_in_sem.at[side],
            device_id={"hour": to},
        )

    def near_copy(side, half, to):
        return pltpu.make_async_remote_copy(
            near_out.at[side, half], near_in.at[side, half],
            near_out_sem.at[side, half], near_in_sem.at[side, half], device_id={"hour": to},
        )

    def piece(step, carry):
        order = jnp.where(step < 2, 0, jnp.where(step >= 6, 3, 1 + lax.rem(step, 2)))
        half = jnp.where((step == 2) | (step == 3), 3 - step, lax.rem(step, 2))

        for at, which in ((0, 0), (2, 1), (3, 2), (6, 3)):
            @pl.when(step == at)
            def _():
                arrive(which)

        half_stack(source_ref, white_ref, table_ref, total_ref, order, half * GROUP)

        for side, to in ((0, above), (1, below)):
            @pl.when(step == side)
            def _():
                far_out[side] = (total_ref[...] * scale).astype(jnp.bfloat16)
                far_copy(side, to).start()

            @pl.when(step == 2 + side)
            def _():
                near_out[side, 1 - side] = (total_ref[...] * scale).astype(jnp.bfloat16)
                near_copy(side, 1 - side, to).start()

            @pl.when(step == 4 + side)
            def _():
                far_copy(side, to).wait_recv()
                near_out[side, side] = (
                    total_ref[...] * scale + far_in[side].astype(jnp.float32)
                ).astype(jnp.bfloat16)
                near_copy(side, side, to).start()

            @pl.when(step == 6 + side)
            def _():
                out_ref[side] = total_ref[...] * scale

        return carry

    lax.fori_loop(0, 8, piece, 0)
    for side in (1, 0):
        near_copy(1 - side, side, above).wait_recv()
        near_copy(side, side, above).wait_recv()
        out_ref[side] += near_in[0, side].astype(jnp.float32) + near_in[1, side].astype(jnp.float32)

    others = chunk_ref.at[pl.ds(0, blocks - 1)]
    pltpu.make_async_copy(others, others, spread_out).wait()
    for order in range(hours):
        part = chosen_ref.at[order, pl.ds(0, blocks - 1)]
        pltpu.make_async_copy(part, part, slot_out.at[order]).wait()
    for side in range(2):
        far_copy(side, above).wait_send()
        for half in range(2):
            near_copy(side, half, above).wait_send()


def fused(wanted, spectra, table, scale, hours):
    blocks, slots = wanted.shape
    rows = GROUP * CH
    bf16 = jnp.bfloat16
    dma = pltpu.SemaphoreType.DMA
    return pl.pallas_call(
        functools.partial(fused_kernel, scale, blocks, hours),
        out_shape=jax.ShapeDtypeStruct((2, rows, LAGS), jnp.float32),
        in_specs=[pl.BlockSpec(memory_space=pltpu.SMEM)] + [pl.BlockSpec(memory_space=pltpu.VMEM)] * 2,
        out_specs=pl.BlockSpec(memory_space=pltpu.VMEM),
        scratch_shapes=[
            pltpu.VMEM((WIN, 2, CH, F), bf16),
            pltpu.VMEM((blocks, 2, FQ), bf16),
            pltpu.VMEM((blocks + 1, 2, FQ), bf16),
            pltpu.VMEM((slots, blocks, 2, FQ), bf16),
            pltpu.VMEM((slots, blocks, 2, FQ), bf16),
            pltpu.VMEM((rows, LAGS), jnp.float32),
            pltpu.VMEM((2, rows, LAGS), bf16),
            pltpu.VMEM((2, rows, LAGS), bf16),
            pltpu.VMEM((2, 2, rows, LAGS), bf16),
            pltpu.VMEM((2, 2, rows, LAGS), bf16),
            dma, dma, dma((slots,)), dma((slots,)), dma((2,)), dma((2,)), dma((2, 2)), dma((2, 2)),
        ],
        compiler_params=pltpu.CompilerParams(
            collective_id=0, has_side_effects=True, vmem_limit_bytes=50 << 20
        ),
    )(wanted, spectra, table)


def slot_sources(partner_lists, partner_counts):
    blocks, most = partner_lists.shape
    offsets = jnp.arange(most, dtype=jnp.int32)
    live = offsets[None, :] < partner_counts[:, None]
    receivers = jnp.arange(blocks, dtype=jnp.int32)
    member = jnp.any((partner_lists[None] == receivers[:, None, None]) & live[None], 2)
    below = receivers[:, None] < receivers[None, :]
    rank = jnp.sum(member[:, :, None] & below[None], 1, dtype=jnp.int32)
    hit = member[:, None, :] & (rank[:, None, :] == offsets[None, :, None])
    source = jnp.sum(jnp.where(hit, receivers[None, None, :], 0), 2, dtype=jnp.int32)
    return jnp.where(jnp.any(hit, 2), source, blocks)


def shards(spectra, partner_lists, partner_counts):
    hours = lax.axis_size("hour")
    scale = 1.0 / math.sqrt(4.0 * F * WIN * hours)
    wanted = slot_sources(partner_lists, partner_counts)
    stacks = fused(wanted, spectra, jnp.asarray(lag_table()), scale, hours)
    return stacks.reshape(1, VS, CH, LAGS)


def solution(mesh):
    return jax.shard_map(
        shards,
        mesh=mesh,
        in_specs=(P("hour", None, "chan", None), P(), P()),
        out_specs=P(("chan", "hour"), None, None, None),
        check_vma=False,
    )
```

time: 117 us -> 56.7 us (0.48)
  blocking collectives: 55 us -> 0 us
  Pallas kernels: 20.3 us -> 51.1 us
  starting transfers between devices: 13.2 us -> 0 us
  other arithmetic: 12.5 us -> 2.45 us
  waiting for transfers between devices: 9.18 us -> 0 us
  local copies, waits for them, and re-layouts: 6.28 us -> 2.92 us
    all_to_all x2 -> x0, blocking collectives: 55 us -> none  [the longest x1 29.7 us: shards(): hourly = lax.all_to_all(partial, 'hour', 0, 0, tiled=True)]
    pallas_call x2 -> x1, Pallas kernels: 20.3 us -> 51.1 us  [fused(): pl.pallas_call(functools.partial(fused_kernel, scale, blocks, hours), out...]
    all_to_all x1 -> x0, starting transfers between devices: 13.2 us -> none  [shards(): mine = lax.all_to_all(chunks, 'chan', 0, 0, tiled=True)]
    all_to_all x3 -> x0, other arithmetic: 10 us -> none  [the longest x2 8.47 us: shards(): arrived = lax.all_to_all(chosen, 'chan', 0, 0, tiled=True)]
    all_to_all x1 -> x0, waiting for transfers between devices: 9.18 us -> none  [shards(): mine = lax.all_to_all(chunks, 'chan', 0, 0, tiled=True)]
    reduce_sum x1 -> x0, other arithmetic: 1.31 us -> none  [shards(): total = jnp.sum(hourly.astype(jnp.float32), 0)]
    gather x1 -> x0, local copies, waits for them, and re-layouts: 1.25 us -> none  [shards(): chosen = mine[wanted.reshape(-1)].reshape(blocks, slots * 2 * FQ)]
    unnamed x11 -> x3, local copies, waits for them, and re-layouts: 3.37 us -> 2.71 us
  transfers between devices with their start and end apart: 1 -> 0, of which waited for: 1 -> 0; matrix products, arithmetic and copies ran while one was open for 1% -> 0% of each run, Pallas kernels for 0% -> 0%
where the time goes in v2:
time: 56.7 us; the launch traced here: 56.5 us
  Pallas kernels  51.1 us (90%)
  local copies, waits for them, and re-layouts  2.92 us (5%)
  other arithmetic  2.45 us (4%)
    pallas_call x1, Pallas kernels, fused(): pl.pallas_call(functools.partial(fused_kernel, scale, blocks, hours), out...  51.1 us
    unnamed x3, local copies, waits for them, and re-layouts  2.71 us

profile of v2, /device:TPU:1, one launch (start us, length us, event | category | flops | bytes accessed | tf_op | source)
XLA Modules:
  0.0 56.5 jit_solution(1747417783991683991)
XLA Ops:
  0.0 0.7 %iota_compare_fusion.3 = pred[64,4]{0,1:T(4,128)(4,1)S(1)} fusion(s32[64]{0:T(128)} %param.6), kind=kLoop, calls=%fused_computation.10 | loop fusion | flops 256 | bytes 512 | tf_op jit(solution)/shard_map/lt | solution.py:278
  0.7 0.7 %fusion.1 = pred[64,64]{1,0:T(8,128)(4,1)S(1)} fusion(s32[64,4]{0,1:T(4,128)} %param.5, pred[64,4]{0,1:T(4,128)(4,1)S(1)} %iota_compare_fusion.3), kind=kLoop, calls=%fused_computation.5 | loop fusion | flops 45056 | bytes 5376 | tf_op jit(solution)/shard_map/reduce_or | solution.py:280
  1.4 0.8 %convert_reduce_fusion = s32[64,64]{1,0:T(8,128)S(1)} fusion(pred[64,64]{1,0:T(8,128)(4,1)S(1)} %iota_compare_fusion.2, pred[64,64]{1,0:T(8,128)(4,1)S(1)} %fusion.1), kind=kLoop, calls=%fused_computation | loop fusion | flops 782336 | bytes 24576 | tf_op jit(solution)/shard_map/reduce_sum | solution.py:282
  2.2 0.1 fusion.3
  2.3 0.2 select_reduce_fusion
  2.5 0.1 copy.6
  2.6 0.1 copy.7
  2.7 0.0 copy-start
  2.7 1.7 %copy-done = bf16[2,2,128,2560]{3,2,1,0:T(8,128)(2,1)S(1)} copy-done((bf16[2,2,128,2560]{3,2,1,0:T(8,128)(2,1)S(1)}, bf16[2,2,128,2560]{3,2,1,0:T(8,128)(2,1)}, u32[]{:S(2)}) %copy-start) | copy-done | bytes 2621464
  4.4 51.1 %shard_map.46 = f32[2,512,256]{2,1,0:T(8,128)S(1)} custom-call(s32[64,4]{1,0:T(8,128)S(1)} %broadcast_select_fusion.wanted_ref, bf16[2,2,128,2560]{3,2,1,0:T(8,128)(2,1)S(1)} %copy-done, bf16[4,1280,256]{2,1,0:T(8,128)(2,1)} %constant.8.clone.table_ref), custom_call_target="tpu_custom_call" | custom-call | tf_op jit(solution)/shard_map/pallas_call | solution.py:251
  55.6 1.0 %copy.9 = f32[1,8,128,256]{3,2,1,0:T(8,128)} copy(f32[1,8,128,256]{3,2,1,0:T(8,128)S(1)} %bitcast.1) | data formatting | bytes 2097152
  (2 shorter events, 0.0 us)
Async XLA Ops:
  2.7 1.7 %copy-start = (bf16[2,2,128,2560]{3,2,1,0:T(8,128)(2,1)S(1)}, bf16[2,2,128,2560]{3,2,1,0:T(8,128)(2,1)}, u32[]{:S(2)}) copy-start(bf16[2,2,128,2560]{3,2,1,0:T(8,128)(2,1)} %x_ref.1) | copy-start | bytes 7864324

commit v3 on v2

--- a/solution.py
+++ b/solution.py
@@ -20,7 +20,7 @@
 WIN = 2
 QUARTERS = 4
 FQ = F // QUARTERS
-GROUP = 4
+GROUP = 2
 
 
 def lag_table():
@@ -88,7 +88,7 @@
                     chunk_ref[(v * WIN + w) * QUARTERS + q, p:p + 1, :] = one
 
 
-def half_stack(source_ref, white_ref, table_ref, total_ref, order, first):
+def piece_stack(source_ref, white_ref, table_ref, total_ref, order, first):
     for q in range(QUARTERS):
         bins = slice(q * FQ, (q + 1) * FQ)
         xr = [white_ref[w, 0, :, bins].reshape(8, 16, FQ) for w in range(WIN)]
@@ -115,10 +115,11 @@
 
 
 def fused_kernel(
-    scale, blocks, hours, wanted_ref, x_ref, table_ref, out_ref,
-    white_ref, chunk_ref, mine_ref, chosen_ref, source_ref, total_ref,
-    far_out, far_in, near_out, near_in,
-    spread_out, spread_in, slot_out, slot_in, far_out_sem, far_in_sem, near_out_sem, near_in_sem,
+    scale, blocks, hours, lists_ref, counts_ref, x_any, table_any, out_ref,
+    x_ref, table_ref, white_ref, wanted_vec, wanted_ref, chunk_ref, mine_ref, chosen_ref,
+    source_ref, total_ref, far_out, far_in, near_out, near_in,
+    load_sem, spread_out, spread_in, slot_out, slot_in,
+    far_out_sem, far_in_sem, near_out_sem, near_in_sem,
 ):
     me = lax.axis_index("chan")
     hour = lax.axis_index("hour")
@@ -130,14 +131,24 @@
         pl.semaphore_signal(barrier, inc=1, device_id={"chan": lax.rem(me + k, blocks)})
         return carry
 
+    load_x = pltpu.make_async_copy(x_any, x_ref, load_sem.at[0])
+    load_table = pltpu.make_async_copy(table_any, table_ref, load_sem.at[1])
+    load_wanted = pltpu.make_async_copy(wanted_vec, wanted_ref, load_sem.at[2])
+    load_x.start()
     lax.fori_loop(1, blocks, greet, 0)
     for to in (above, below):
         pl.semaphore_signal(barrier, inc=1, device_id={"hour": to})
-
+    load_table.start()
+
+    wanted_vec[...] = slot_table(lists_ref, counts_ref, blocks)
+    load_wanted.start()
     band = band_matrix()
+    load_x.wait()
     whiten_sources(x_ref, chunk_ref, band)
     mine_ref[blocks] = jnp.zeros(mine_ref.shape[1:], jnp.bfloat16)
     mine_ref[me] = chunk_ref[me]
+    whiten_window(x_ref, white_ref, band, 0)
+    load_wanted.wait()
     pl.semaphore_wait(barrier, blocks + 1)
 
     def spread(k, carry):
@@ -148,12 +159,16 @@
         return carry
 
     lax.fori_loop(1, blocks, spread, 0)
-    whiten_window(x_ref, white_ref, band, 0)
+    whiten_window(x_ref, white_ref, band, 1)
     others = mine_ref.at[pl.ds(0, blocks - 1)]
     pltpu.make_async_copy(others, others, spread_in).wait()
 
+    upper = me // (blocks // 2)
+
     def slot_of(order):
-        return lax.rem(hour + jnp.where(order == 0, 2, jnp.where(order == 3, 0, 2 * order - 1)), hours)
+        side = lax.rem(order + upper, 2)
+        away = jnp.where(order == 0, 2, jnp.where(order == 3, 0, jnp.where(side == 0, 1, 3)))
+        return lax.rem(hour + away, hours)
 
     def choose(order, carry):
         slot = slot_of(order)
@@ -172,65 +187,68 @@
         return carry
 
     lax.fori_loop(0, hours, choose, 0)
-    whiten_window(x_ref, white_ref, band, 1)
-
-    def arrive(order):
-        part = source_ref.at[order, pl.ds(0, blocks - 1)]
-        pltpu.make_async_copy(part, part, slot_in.at[order]).wait()
-
-    def far_copy(side, to):
+    load_table.wait()
+
+    def far_copy(side, sub):
         return pltpu.make_async_remote_copy(
-            far_out.at[side], far_in.at[side], far_out_sem.at[side], far_in_sem.at[side],
-            device_id={"hour": to},
+            far_out.at[side, sub], far_in.at[side, sub],
+            far_out_sem.at[side, sub], far_in_sem.at[side, sub],
+            device_id={"hour": jnp.where(side == 0, above, below)},
         )
 
-    def near_copy(side, half, to):
+    def near_copy(side, half, sub):
         return pltpu.make_async_remote_copy(
-            near_out.at[side, half], near_in.at[side, half],
-            near_out_sem.at[side, half], near_in_sem.at[side, half], device_id={"hour": to},
+            near_out.at[side, half, sub], near_in.at[side, half, sub],
+            near_out_sem.at[side, half, sub], near_in_sem.at[side, half, sub],
+            device_id={"hour": jnp.where(side == 0, above, below)},
         )
 
     def piece(step, carry):
-        order = jnp.where(step < 2, 0, jnp.where(step >= 6, 3, 1 + lax.rem(step, 2)))
-        half = jnp.where((step == 2) | (step == 3), 3 - step, lax.rem(step, 2))
-
-        for at, which in ((0, 0), (2, 1), (3, 2), (6, 3)):
-            @pl.when(step == at)
-            def _():
-                arrive(which)
-
-        half_stack(source_ref, white_ref, table_ref, total_ref, order, half * GROUP)
-
-        for side, to in ((0, above), (1, below)):
-            @pl.when(step == side)
-            def _():
-                far_out[side] = (total_ref[...] * scale).astype(jnp.bfloat16)
-                far_copy(side, to).start()
-
-            @pl.when(step == 2 + side)
-            def _():
-                near_out[side, 1 - side] = (total_ref[...] * scale).astype(jnp.bfloat16)
-                near_copy(side, 1 - side, to).start()
-
-            @pl.when(step == 4 + side)
-            def _():
-                far_copy(side, to).wait_recv()
-                near_out[side, side] = (
-                    total_ref[...] * scale + far_in[side].astype(jnp.float32)
-                ).astype(jnp.bfloat16)
-                near_copy(side, side, to).start()
-
-            @pl.when(step == 6 + side)
-            def _():
-                out_ref[side] = total_ref[...] * scale
+        order = step // 4
+        sub = lax.rem(step // 2, 2)
+        side = lax.rem(step, 2)
+        half = jnp.where(order == 1, 1 - side, side)
+
+        @pl.when(lax.rem(step, 4) == 0)
+        def _():
+            part = source_ref.at[order, pl.ds(0, blocks - 1)]
+            pltpu.make_async_copy(part, part, slot_in.at[order]).wait()
+
+        piece_stack(source_ref, white_ref, table_ref, total_ref, order, (half * 2 + sub) * GROUP)
+
+        @pl.when(order == 0)
+        def _():
+            far_out[side, sub] = (total_ref[...] * scale).astype(jnp.bfloat16)
+            far_copy(side, sub).start()
+
+        @pl.when(order == 1)
+        def _():
+            near_out[side, half, sub] = (total_ref[...] * scale).astype(jnp.bfloat16)
+            near_copy(side, half, sub).start()
+
+        @pl.when(order == 2)
+        def _():
+            far_copy(side, sub).wait_recv()
+            near_out[side, half, sub] = (
+                total_ref[...] * scale + far_in[side, sub].astype(jnp.float32)
+            ).astype(jnp.bfloat16)
+            near_copy(side, half, sub).start()
+
+        @pl.when(order == 3)
+        def _():
+            out_ref[half, sub] = total_ref[...] * scale
 
         return carry
 
-    lax.fori_loop(0, 8, piece, 0)
-    for side in (1, 0):
-        near_copy(1 - side, side, above).wait_recv()
-        near_copy(side, side, above).wait_recv()
-        out_ref[side] += near_in[0, side].astype(jnp.float32) + near_in[1, side].astype(jnp.float32)
+    lax.fori_loop(0, 16, piece, 0)
+    for sub in range(2):
+        for half in range(2):
+            near_copy(1 - half, half, sub).wait_recv()
+            near_copy(half, half, sub).wait_recv()
+            out_ref[half, sub] += (
+                near_in[0, half, sub].astype(jnp.float32)
+                + near_in[1, half, sub].astype(jnp.float32)
+            )
 
     others = chunk_ref.at[pl.ds(0, blocks - 1)]
     pltpu.make_async_copy(others, others, spread_out).wait()
@@ -238,58 +256,76 @@
         part = chosen_ref.at[order, pl.ds(0, blocks - 1)]
         pltpu.make_async_copy(part, part, slot_out.at[order]).wait()
     for side in range(2):
-        far_copy(side, above).wait_send()
-        for half in range(2):
-            near_copy(side, half, above).wait_send()
-
-
-def fused(wanted, spectra, table, scale, hours):
-    blocks, slots = wanted.shape
+        for sub in range(2):
+            far_copy(side, sub).wait_send()
+            for half in range(2):
+                near_copy(side, half, sub).wait_send()
+
+
+def fused(lists, counts, spectra, table, scale, hours):
+    slots, blocks = lists.shape
+    lists = jnp.pad(lists, ((0, 0), (0, 128 - blocks)), constant_values=-1)
+    counts = jnp.pad(counts[None], ((0, 0), (0, 128 - blocks)))
     rows = GROUP * CH
     bf16 = jnp.bfloat16
     dma = pltpu.SemaphoreType.DMA
+    vmem = pl.BlockSpec(memory_space=pltpu.VMEM)
+    leave = pl.BlockSpec(memory_space=pltpu.HBM)
     return pl.pallas_call(
         functools.partial(fused_kernel, scale, blocks, hours),
-        out_shape=jax.ShapeDtypeStruct((2, rows, LAGS), jnp.float32),
-        in_specs=[pl.BlockSpec(memory_space=pltpu.SMEM)] + [pl.BlockSpec(memory_space=pltpu.VMEM)] * 2,
-        out_specs=pl.BlockSpec(memory_space=pltpu.VMEM),
+        out_shape=jax.ShapeDtypeStruct((2, 2, rows, LAGS), jnp.float32),
+        in_specs=[vmem, vmem, leave, leave],
+        out_specs=vmem,
         scratch_shapes=[
+            pltpu.VMEM(spectra.shape, bf16),
+            pltpu.VMEM(table.shape, bf16),
             pltpu.VMEM((WIN, 2, CH, F), bf16),
+            pltpu.VMEM((blocks, 128), jnp.int32),
+            pltpu.SMEM((blocks, 128), jnp.int32),
             pltpu.VMEM((blocks, 2, FQ), bf16),
             pltpu.VMEM((blocks + 1, 2, FQ), bf16),
             pltpu.VMEM((slots, blocks, 2, FQ), bf16),
             pltpu.VMEM((slots, blocks, 2, FQ), bf16),
             pltpu.VMEM((rows, LAGS), jnp.float32),
-            pltpu.VMEM((2, rows, LAGS), bf16),
-            pltpu.VMEM((2, rows, LAGS), bf16),
             pltpu.VMEM((2, 2, rows, LAGS), bf16),
             pltpu.VMEM((2, 2, rows, LAGS), bf16),
-            dma, dma, dma((slots,)), dma((slots,)), dma((2,)), dma((2,)), dma((2, 2)), dma((2, 2)),
+            pltpu.VMEM((2, 2, 2, rows, LAGS), bf16),
+            pltpu.VMEM((2, 2, 2, rows, LAGS), bf16),
+            dma((3,)), dma, dma, dma((slots,)), dma((slots,)),
+            dma((2, 2)), dma((2, 2)), dma((2, 2, 2)), dma((2, 2, 2)),
         ],
         compiler_params=pltpu.CompilerParams(
             collective_id=0, has_side_effects=True, vmem_limit_bytes=50 << 20
         ),
-    )(wanted, spectra, table)
-
-
-def slot_sources(partner_lists, partner_counts):
-    blocks, most = partner_lists.shape
-    offsets = jnp.arange(most, dtype=jnp.int32)
-    live = offsets[None, :] < partner_counts[:, None]
-    receivers = jnp.arange(blocks, dtype=jnp.int32)
-    member = jnp.any((partner_lists[None] == receivers[:, None, None]) & live[None], 2)
-    below = receivers[:, None] < receivers[None, :]
-    rank = jnp.sum(member[:, :, None] & below[None], 1, dtype=jnp.int32)
-    hit = member[:, None, :] & (rank[:, None, :] == offsets[None, :, None])
-    source = jnp.sum(jnp.where(hit, receivers[None, None, :], 0), 2, dtype=jnp.int32)
-    return jnp.where(jnp.any(hit, 2), source, blocks)
+    )(lists, counts, spectra, table)
+
+
+def slot_table(lists_ref, counts_ref, blocks):
+    most = lists_ref.shape[0]
+    shape = (blocks, 128)
+    receiver = lax.broadcasted_iota(jnp.int32, shape, 0)
+    lane = lax.broadcasted_iota(jnp.int32, shape, 1)
+    counts = jnp.broadcast_to(counts_ref[...], shape)
+    member = jnp.zeros(shape, jnp.int32)
+    for offset in range(most):
+        listed = jnp.broadcast_to(lists_ref[offset:offset + 1, :], shape) == receiver
+        member = jnp.where(listed & (offset < counts), 1, member)
+    rank = member
+    for step in (1, 2, 4, 8, 16, 32):
+        rank = rank + jnp.where(lane >= step, pltpu.roll(rank, step, 1), 0)
+    table = jnp.zeros(shape, jnp.int32)
+    for slot in range(most):
+        hit = (member > 0) & (rank == slot + 1)
+        source = jnp.sum(jnp.where(hit, lane - blocks, 0), axis=1, keepdims=True) + blocks
+        table = jnp.where(lane == slot, source, table)
+    return table
 
 
 def shards(spectra, partner_lists, partner_counts):
     hours = lax.axis_size("hour")
     scale = 1.0 / math.sqrt(4.0 * F * WIN * hours)
-    wanted = slot_sources(partner_lists, partner_counts)
-    stacks = fused(wanted, spectra, jnp.asarray(lag_table()), scale, hours)
+    table = jnp.asarray(lag_table())
+    stacks = fused(partner_lists.T, partner_counts, spectra, table, scale, hours)
     return stacks.reshape(1, VS, CH, LAGS)
 
 

time: 56.7 us -> 52.7 us (0.929)
  Pallas kernels: 51.1 us -> 48.5 us
  other arithmetic: 2.45 us -> 0 us
  local copies, waits for them, and re-layouts: 2.92 us -> 4.06 us
    pallas_call x1, Pallas kernels: 51.1 us -> 48.5 us  [fused(): pl.pallas_call(functools.partial(fused_kernel, scale, blocks, hours), out...]
    pad x0 -> x2, local copies, waits for them, and re-layouts: none -> 1.35 us  [the longest x1 0.69 us: fused(): lists = jnp.pad(lists, ((0, 0), (0, 128 - blocks)), constant_values=-1)]
    reduce_sum x2 -> x0, other arithmetic: 0.91 us -> none  [the longest x1 0.76 us: slot_sources(): rank = jnp.sum(member[:, :, None] & below[None], 1, dtype=jnp.int32)]
    reduce_or x2 -> x0, other arithmetic: 0.86 us -> none  [the longest x1 0.71 us: slot_sources(): jnp.any((partner_lists[None] == receivers[:, None, None]) & live[None], 2)]
    lt x2 -> x0, other arithmetic: 0.67 us -> none  [the longest x1 0.66 us: slot_sources(): live = offsets[None, :] < partner_counts[:, None]]
where the time goes in v3:
time: 52.7 us; the launch traced here: 52.5 us
  Pallas kernels  48.5 us (92%)
  local copies, waits for them, and re-layouts  4.06 us (8%)
    pallas_call x1, Pallas kernels, fused(): pl.pallas_call(functools.partial(fused_kernel, scale, blocks, hours), out...  48.5 us
    unnamed x3, local copies, waits for them, and re-layouts  2.71 us

profile of v3, /device:TPU:1, one launch (start us, length us, event | category | flops | bytes accessed | tf_op | source)
XLA Modules:
  0.0 52.5 jit_solution(11400871733569440373)
XLA Ops:
  0.0 0.7 %pad.9.counts_ref = s32[1,128]{1,0:T(1,128)S(1)} pad(s32[1,64]{1,0:T(1,128)} %bitcast.5, s32[]{:T(128)} %constant.2.clone.1), padding=0_0x0_64 | pad | bytes 772 | tf_op jit(solution)/shard_map/jit(_pad)/pad | solution.py:268
  0.7 0.7 %pad.8.lists_ref = s32[4,128]{1,0:T(4,128)S(1)} pad(s32[4,64]{1,0:T(4,128)} %bitcast.4, s32[]{:T(128)} %constant.1.clone.1), padding=0_0x0_64 | pad | bytes 3076 | tf_op jit(solution)/shard_map/jit(_pad)/pad | solution.py:267
  1.3 0.0 copy-start
  1.3 1.7 %copy-done = bf16[2,2,128,2560]{3,2,1,0:T(8,128)(2,1)S(1)} copy-done((bf16[2,2,128,2560]{3,2,1,0:T(8,128)(2,1)S(1)}, bf16[2,2,128,2560]{3,2,1,0:T(8,128)(2,1)}, u32[]{:S(2)}) %copy-start) | copy-done | bytes 2621464
  3.1 48.5 %shard_map.46 = f32[2,2,256,256]{3,2,1,0:T(8,128)S(1)} custom-call(s32[4,128]{1,0:T(4,128)S(1)} %pad.8.lists_ref, s32[1,128]{1,0:T(1,128)S(1)} %pad.9.counts_ref, bf16[2,2,128,2560]{3,2,1,0:T(8,128)(2,1)S(1)} %copy-done, bf16[4,1280,256]{2,1,0:T(8,128)(2,1)} %constant.6.clone.table_any), custom_call_target="tpu_custom_call" | custom-call | tf_op jit(solution)/shard_map/pallas_call | solution.py:274
  51.6 1.0 %copy.6 = f32[1,8,128,256]{3,2,1,0:T(8,128)} copy(f32[1,8,128,256]{3,2,1,0:T(8,128)S(1)} %bitcast.3) | data formatting | bytes 2097152
Async XLA Ops:
  1.3 1.7 %copy-start = (bf16[2,2,128,2560]{3,2,1,0:T(8,128)(2,1)S(1)}, bf16[2,2,128,2560]{3,2,1,0:T(8,128)(2,1)}, u32[]{:S(2)}) copy-start(bf16[2,2,128,2560]{3,2,1,0:T(8,128)(2,1)} %x_any.1) | copy-start | bytes 7864324

commit v4 on v3

--- a/solution.py
+++ b/solution.py
@@ -69,6 +69,11 @@
         inverse = inverse_mean(real, imag, band)
         white_ref[w, 0, c:c + 64, :] = (real * inverse).astype(jnp.bfloat16)
         white_ref[w, 1, c:c + 64, :] = (imag * inverse).astype(jnp.bfloat16)
+
+
+def chunk_place(v, w, q):
+    pair = v // 2
+    return pair % 2, ((pair // 2 * 2 + v % 2) * WIN + w) * QUARTERS + q
 
 
 def whiten_sources(x_ref, chunk_ref, band):
@@ -85,10 +90,11 @@
                 row = w * VS + v
                 for q in range(QUARTERS):
                     one = white[row:row + 1, q * FQ:(q + 1) * FQ].astype(jnp.bfloat16)
-                    chunk_ref[(v * WIN + w) * QUARTERS + q, p:p + 1, :] = one
-
-
-def piece_stack(source_ref, white_ref, table_ref, total_ref, order, first):
+                    core, place = chunk_place(v, w, q)
+                    chunk_ref[core, place, p:p + 1, :] = one
+
+
+def piece_stack(source_ref, white_ref, table_ref, total_ref, order, half, sub):
     for q in range(QUARTERS):
         bins = slice(q * FQ, (q + 1) * FQ)
         xr = [white_ref[w, 0, :, bins].reshape(8, 16, FQ) for w in range(WIN)]
@@ -97,8 +103,8 @@
         for v in range(GROUP):
             s = []
             for w in range(WIN):
-                chunk = ((first + v) * WIN + w) * QUARTERS + q
-                both = source_ref[order, chunk].astype(jnp.float32)
+                place = ((half * 2 + v) * WIN + w) * QUARTERS + q
+                both = source_ref[order, sub, place].astype(jnp.float32)
                 for p in range(2):
                     one = jnp.broadcast_to(both[p:p + 1], (16, FQ))
                     s.append(one.astype(jnp.bfloat16)[None])
@@ -116,12 +122,15 @@
 
 def fused_kernel(
     scale, blocks, hours, lists_ref, counts_ref, x_any, table_any, out_ref,
-    x_ref, table_ref, white_ref, wanted_vec, wanted_ref, chunk_ref, mine_ref, chosen_ref,
+    x_ref, table_ref, white_ref, padded_ref, wanted_vec, wanted_ref, chunk_ref, mine_ref, chosen_ref,
     source_ref, total_ref, far_out, far_in, near_out, near_in,
     load_sem, spread_out, spread_in, slot_out, slot_in,
     far_out_sem, far_in_sem, near_out_sem, near_in_sem,
 ):
     me = lax.axis_index("chan")
+    core = lax.rem(me, 2)
+    chip = me // 2
+    chips = blocks // 2
     hour = lax.axis_index("hour")
     above = lax.rem(hour + 1, hours)
     below = lax.rem(hour + hours - 1, hours)
@@ -140,25 +149,32 @@
         pl.semaphore_signal(barrier, inc=1, device_id={"hour": to})
     load_table.start()
 
-    wanted_vec[...] = slot_table(lists_ref, counts_ref, blocks)
+    wanted_vec[...] = slot_table(lists_ref, counts_ref, padded_ref, blocks)
     load_wanted.start()
     band = band_matrix()
     load_x.wait()
     whiten_sources(x_ref, chunk_ref, band)
     mine_ref[blocks] = jnp.zeros(mine_ref.shape[1:], jnp.bfloat16)
-    mine_ref[me] = chunk_ref[me]
+    mine_ref[me] = chunk_ref[core, chip]
     whiten_window(x_ref, white_ref, band, 0)
     load_wanted.wait()
     pl.semaphore_wait(barrier, blocks + 1)
 
-    def spread(k, carry):
-        to = lax.rem(me + k, blocks)
-        pltpu.make_async_remote_copy(
-            chunk_ref.at[to], mine_ref.at[me], spread_out, spread_in, device_id={"chan": to}
-        ).start()
-        return carry
-
-    lax.fori_loop(1, blocks, spread, 0)
+    for kind in range(2):
+        def spread(k, carry):
+            to = lax.rem(chip + k, chips)
+
+            @pl.when((k > 0) | (core != kind))
+            def _():
+                pltpu.make_async_remote_copy(
+                    chunk_ref.at[kind, to], mine_ref.at[me], spread_out, spread_in,
+                    device_id={"chan": to * 2 + kind},
+                ).start()
+
+            return carry
+
+        lax.fori_loop(0, chips, spread, 0)
+
     whiten_window(x_ref, white_ref, band, 1)
     others = mine_ref.at[pl.ds(0, blocks - 1)]
     pltpu.make_async_copy(others, others, spread_in).wait()
@@ -177,13 +193,13 @@
             to = lax.rem(me + k, blocks)
             chosen_ref[order, to] = mine_ref[wanted_ref[to, slot]]
             pltpu.make_async_remote_copy(
-                chosen_ref.at[order, to], source_ref.at[order, me],
-                slot_out.at[order], slot_in.at[order], device_id={"chan": to},
+                chosen_ref.at[order, to], source_ref.at[order, core, chip],
+                slot_out.at[order], slot_in.at[order, core], device_id={"chan": to},
             ).start()
             return inner
 
         lax.fori_loop(1, blocks, one, 0)
-        source_ref[order, me] = mine_ref[wanted_ref[me, slot]]
+        source_ref[order, core, chip] = mine_ref[wanted_ref[me, slot]]
         return carry
 
     lax.fori_loop(0, hours, choose, 0)
@@ -209,12 +225,19 @@
         side = lax.rem(step, 2)
         half = jnp.where(order == 1, 1 - side, side)
 
-        @pl.when(lax.rem(step, 4) == 0)
-        def _():
-            part = source_ref.at[order, pl.ds(0, blocks - 1)]
-            pltpu.make_async_copy(part, part, slot_in.at[order]).wait()
-
-        piece_stack(source_ref, white_ref, table_ref, total_ref, order, (half * 2 + sub) * GROUP)
+        @pl.when(lax.rem(step, 2) == 0)
+        def _():
+            @pl.when(sub == core)
+            def _():
+                part = source_ref.at[order, sub, pl.ds(0, chips - 1)]
+                pltpu.make_async_copy(part, part, slot_in.at[order, sub]).wait()
+
+            @pl.when(sub != core)
+            def _():
+                part = source_ref.at[order, sub]
+                pltpu.make_async_copy(part, part, slot_in.at[order, sub]).wait()
+
+        piece_stack(source_ref, white_ref, table_ref, total_ref, order, half, sub)
 
         @pl.when(order == 0)
         def _():
@@ -250,7 +273,6 @@
                 + near_in[1, half, sub].astype(jnp.float32)
             )
 
-    others = chunk_ref.at[pl.ds(0, blocks - 1)]
     pltpu.make_async_copy(others, others, spread_out).wait()
     for order in range(hours):
         part = chosen_ref.at[order, pl.ds(0, blocks - 1)]
@@ -264,8 +286,6 @@
 
 def fused(lists, counts, spectra, table, scale, hours):
     slots, blocks = lists.shape
-    lists = jnp.pad(lists, ((0, 0), (0, 128 - blocks)), constant_values=-1)
-    counts = jnp.pad(counts[None], ((0, 0), (0, 128 - blocks)))
     rows = GROUP * CH
     bf16 = jnp.bfloat16
     dma = pltpu.SemaphoreType.DMA
@@ -280,35 +300,39 @@
             pltpu.VMEM(spectra.shape, bf16),
             pltpu.VMEM(table.shape, bf16),
             pltpu.VMEM((WIN, 2, CH, F), bf16),
+            pltpu.VMEM((8, 128), jnp.int32),
             pltpu.VMEM((blocks, 128), jnp.int32),
             pltpu.SMEM((blocks, 128), jnp.int32),
-            pltpu.VMEM((blocks, 2, FQ), bf16),
+            pltpu.VMEM((2, blocks // 2, 2, FQ), bf16),
             pltpu.VMEM((blocks + 1, 2, FQ), bf16),
             pltpu.VMEM((slots, blocks, 2, FQ), bf16),
-            pltpu.VMEM((slots, blocks, 2, FQ), bf16),
+            pltpu.VMEM((slots, 2, blocks // 2, 2, FQ), bf16),
             pltpu.VMEM((rows, LAGS), jnp.float32),
             pltpu.VMEM((2, 2, rows, LAGS), bf16),
             pltpu.VMEM((2, 2, rows, LAGS), bf16),
             pltpu.VMEM((2, 2, 2, rows, LAGS), bf16),
             pltpu.VMEM((2, 2, 2, rows, LAGS), bf16),
-            dma((3,)), dma, dma, dma((slots,)), dma((slots,)),
+            dma((3,)), dma, dma, dma((slots,)), dma((slots, 2)),
             dma((2, 2)), dma((2, 2)), dma((2, 2, 2)), dma((2, 2, 2)),
         ],
         compiler_params=pltpu.CompilerParams(
-            collective_id=0, has_side_effects=True, vmem_limit_bytes=50 << 20
+            collective_id=0, has_side_effects=True, vmem_limit_bytes=52 << 20
         ),
-    )(lists, counts, spectra, table)
-
-
-def slot_table(lists_ref, counts_ref, blocks):
+    )(lists, counts[None], spectra, table)
+
+
+def slot_table(lists_ref, counts_ref, padded_ref, blocks):
     most = lists_ref.shape[0]
     shape = (blocks, 128)
     receiver = lax.broadcasted_iota(jnp.int32, shape, 0)
     lane = lax.broadcasted_iota(jnp.int32, shape, 1)
-    counts = jnp.broadcast_to(counts_ref[...], shape)
+    padded_ref[...] = jnp.full(padded_ref.shape, -1, jnp.int32)
+    padded_ref[:most, :blocks] = lists_ref[...]
+    padded_ref[most:most + 1, :blocks] = counts_ref[...]
+    counts = jnp.broadcast_to(padded_ref[most:most + 1, :], shape)
     member = jnp.zeros(shape, jnp.int32)
     for offset in range(most):
-        listed = jnp.broadcast_to(lists_ref[offset:offset + 1, :], shape) == receiver
+        listed = jnp.broadcast_to(padded_ref[offset:offset + 1, :], shape) == receiver
         member = jnp.where(listed & (offset < counts), 1, member)
     rank = member
     for step in (1, 2, 4, 8, 16, 32):

time: 52.7 us -> 49.7 us (0.943)
  local copies, waits for them, and re-layouts: 4.06 us -> 2.31 us
  Pallas kernels: 48.5 us -> 47.3 us
    pad x2 -> x0, local copies, waits for them, and re-layouts: 1.35 us -> none  [the longest x1 0.69 us: fused(): lists = jnp.pad(lists, ((0, 0), (0, 128 - blocks)), constant_values=-1)]
    pallas_call x1, Pallas kernels: 48.5 us -> 47.3 us  [fused(): pl.pallas_call(functools.partial(fused_kernel, scale, blocks, hours), out...]
    unnamed x3 -> x5, local copies, waits for them, and re-layouts: 2.71 us -> 2.31 us
where the time goes in v4:
time: 49.7 us; the launch traced here: 49.6 us
  Pallas kernels  47.3 us (95%)
  local copies, waits for them, and re-layouts  2.31 us (5%)
    pallas_call x1, Pallas kernels, fused(): pl.pallas_call(functools.partial(fused_kernel, scale, blocks, hours), out...  47.3 us
    unnamed x5, local copies, waits for them, and re-layouts  2.31 us

profile of v4, /device:TPU:1, one launch (start us, length us, event | category | flops | bytes accessed | tf_op | source)
XLA Modules:
  0.0 49.6 jit_solution(2994286155153797129)
XLA Ops:
  0.0 0.0 copy-start
  0.0 0.7 %copy-done = s32[64,4]{0,1:T(4,128)S(1)} copy-done((s32[64,4]{0,1:T(4,128)S(1)}, s32[64,4]{0,1:T(4,128)}, u32[]{:S(2)}) %copy-start) | copy-done | bytes 1048
  0.7 0.0 copy-start.1
  0.7 0.7 %copy-done.1 = s32[64]{0:T(128)S(1)} copy-done((s32[64]{0:T(128)S(1)}, s32[64]{0:T(128)}, u32[]{:S(2)}) %copy-start.1) | copy-done | bytes 280
  1.3 47.3 %shard_map.46 = f32[2,2,256,256]{3,2,1,0:T(8,128)S(1)} custom-call(s32[4,64]{1,0:T(4,128)S(1)} %bitcast.4, s32[1,64]{1,0:T(1,128)S(1)} %bitcast.5, bf16[2,2,128,2560]{3,2,1,0:T(8,128)(2,1)} %x_any.1, bf16[4,1280,256]{2,1,0:T(8,128)(2,1)} %constant.2.clone.table_any), custom_call_target="tpu_custom_call" | custom-call | tf_op jit(solution)/shard_map/pallas_call | solution.py:294
  48.7 1.0 %copy.6 = f32[1,8,128,256]{3,2,1,0:T(8,128)} copy(f32[1,8,128,256]{3,2,1,0:T(8,128)S(1)} %bitcast.3) | data formatting | bytes 2097152
Async XLA Ops:
  0.0 0.7 %copy-start = (s32[64,4]{0,1:T(4,128)S(1)}, s32[64,4]{0,1:T(4,128)}, u32[]{:S(2)}) copy-start(s32[64,4]{0,1:T(4,128)} %param.5) | copy-start | bytes 3076
  0.7 0.7 %copy-start.1 = (s32[64]{0:T(128)S(1)}, s32[64]{0:T(128)}, u32[]{:S(2)}) copy-start(s32[64]{0:T(128)} %param.6) | copy-start | bytes 772

commit v5 on v4

--- a/solution.py
+++ b/solution.py
@@ -175,7 +175,6 @@
 
         lax.fori_loop(0, chips, spread, 0)
 
-    whiten_window(x_ref, white_ref, band, 1)
     others = mine_ref.at[pl.ds(0, blocks - 1)]
     pltpu.make_async_copy(others, others, spread_in).wait()
 
@@ -202,7 +201,16 @@
         source_ref[order, core, chip] = mine_ref[wanted_ref[me, slot]]
         return carry
 
-    lax.fori_loop(0, hours, choose, 0)
+    for stage in range(2):
+        @pl.when(core == stage)
+        def _():
+            choose(0, 0)
+
+        @pl.when(core != stage)
+        def _():
+            whiten_window(x_ref, white_ref, band, 1)
+
+    lax.fori_loop(1, hours, choose, 0)
     load_table.wait()
 
     def far_copy(side, sub):

time: 49.7 us -> 48.3 us (0.972)
  Pallas kernels: 47.3 us -> 45.9 us
    pallas_call x1, Pallas kernels: 47.3 us -> 45.9 us  [fused(): pl.pallas_call(functools.partial(fused_kernel, scale, blocks, hours), out...]
where the time goes in v5:
time: 48.3 us; the launch traced here: 48.2 us
  Pallas kernels  45.9 us (95%)
  local copies, waits for them, and re-layouts  2.31 us (5%)
    pallas_call x1, Pallas kernels, fused(): pl.pallas_call(functools.partial(fused_kernel, scale, blocks, hours), out...  45.9 us
    unnamed x5, local copies, waits for them, and re-layouts  2.31 us

profile of v5, /device:TPU:1, one launch (start us, length us, event | category | flops | bytes accessed | tf_op | source)
XLA Modules:
  0.0 48.2 jit_solution(12085019513349273682)
XLA Ops:
  0.0 0.0 copy-start
  0.0 0.7 %copy-done = s32[64,4]{0,1:T(4,128)S(1)} copy-done((s32[64,4]{0,1:T(4,128)S(1)}, s32[64,4]{0,1:T(4,128)}, u32[]{:S(2)}) %copy-start) | copy-done | bytes 1048
  0.7 0.0 copy-start.1
  0.7 0.7 %copy-done.1 = s32[64]{0:T(128)S(1)} copy-done((s32[64]{0:T(128)S(1)}, s32[64]{0:T(128)}, u32[]{:S(2)}) %copy-start.1) | copy-done | bytes 280
  1.3 45.9 %shard_map.46 = f32[2,2,256,256]{3,2,1,0:T(8,128)S(1)} custom-call(s32[4,64]{1,0:T(4,128)S(1)} %bitcast.4, s32[1,64]{1,0:T(1,128)S(1)} %bitcast.5, bf16[2,2,128,2560]{3,2,1,0:T(8,128)(2,1)} %x_any.1, bf16[4,1280,256]{2,1,0:T(8,128)(2,1)} %constant.2.clone.table_any), custom_call_target="tpu_custom_call" | custom-call | tf_op jit(solution)/shard_map/pallas_call | solution.py:302
  47.2 1.0 %copy.6 = f32[1,8,128,256]{3,2,1,0:T(8,128)} copy(f32[1,8,128,256]{3,2,1,0:T(8,128)S(1)} %bitcast.3) | data formatting | bytes 2097152
Async XLA Ops:
  0.0 0.7 %copy-start = (s32[64,4]{0,1:T(4,128)S(1)}, s32[64,4]{0,1:T(4,128)}, u32[]{:S(2)}) copy-start(s32[64,4]{0,1:T(4,128)} %param.5) | copy-start | bytes 3076
  0.7 0.7 %copy-start.1 = (s32[64]{0:T(128)S(1)}, s32[64]{0:T(128)}, u32[]{:S(2)}) copy-start(s32[64]{0:T(128)} %param.6) | copy-start | bytes 772

commit v6 on v5

--- a/solution.py
+++ b/solution.py
@@ -189,7 +189,7 @@
         slot = slot_of(order)
 
         def one(k, inner):
-            to = lax.rem(me + k, blocks)
+            to = lax.rem(me + k * 9, blocks)
             chosen_ref[order, to] = mine_ref[wanted_ref[to, slot]]
             pltpu.make_async_remote_copy(
                 chosen_ref.at[order, to], source_ref.at[order, core, chip],

time: 48.3 us -> 48 us (level)
  no operation moved by 1% of the time
where the time goes in v6:
time: 48 us; the launch traced here: 47.9 us
  Pallas kernels  45.6 us (95%)
  local copies, waits for them, and re-layouts  2.31 us (5%)
    pallas_call x1, Pallas kernels, fused(): pl.pallas_call(functools.partial(fused_kernel, scale, blocks, hours), out...  45.6 us
    unnamed x5, local copies, waits for them, and re-layouts  2.31 us

profile of v6, /device:TPU:1, one launch (start us, length us, event | category | flops | bytes accessed | tf_op | source)
XLA Modules:
  0.0 47.9 jit_solution(15206629751763816953)
XLA Ops:
  0.0 0.0 copy-start
  0.0 0.7 %copy-done = s32[64,4]{0,1:T(4,128)S(1)} copy-done((s32[64,4]{0,1:T(4,128)S(1)}, s32[64,4]{0,1:T(4,128)}, u32[]{:S(2)}) %copy-start) | copy-done | bytes 1048
  0.7 0.0 copy-start.1
  0.7 0.7 %copy-done.1 = s32[64]{0:T(128)S(1)} copy-done((s32[64]{0:T(128)S(1)}, s32[64]{0:T(128)}, u32[]{:S(2)}) %copy-start.1) | copy-done | bytes 280
  1.3 45.6 %shard_map.46 = f32[2,2,256,256]{3,2,1,0:T(8,128)S(1)} custom-call(s32[4,64]{1,0:T(4,128)S(1)} %bitcast.4, s32[1,64]{1,0:T(1,128)S(1)} %bitcast.5, bf16[2,2,128,2560]{3,2,1,0:T(8,128)(2,1)} %x_any.1, bf16[4,1280,256]{2,1,0:T(8,128)(2,1)} %constant.2.clone.table_any), custom_call_target="tpu_custom_call" | custom-call | tf_op jit(solution)/shard_map/pallas_call | solution.py:302
  46.9 1.0 %copy.6 = f32[1,8,128,256]{3,2,1,0:T(8,128)} copy(f32[1,8,128,256]{3,2,1,0:T(8,128)S(1)} %bitcast.3) | data formatting | bytes 2097152
Async XLA Ops:
  0.0 0.7 %copy-start = (s32[64,4]{0,1:T(4,128)S(1)}, s32[64,4]{0,1:T(4,128)}, u32[]{:S(2)}) copy-start(s32[64,4]{0,1:T(4,128)} %param.5) | copy-start | bytes 3076
  0.7 0.7 %copy-start.1 = (s32[64]{0:T(128)S(1)}, s32[64]{0:T(128)}, u32[]{:S(2)}) copy-start(s32[64]{0:T(128)} %param.6) | copy-start | bytes 772

commit v7 on v6

--- a/solution.py
+++ b/solution.py
@@ -121,7 +121,7 @@
 
 
 def fused_kernel(
-    scale, blocks, hours, lists_ref, counts_ref, x_any, table_any, out_ref,
+    scale, blocks, hours, lists_ref, x_any, table_any, out_ref,
     x_ref, table_ref, white_ref, padded_ref, wanted_vec, wanted_ref, chunk_ref, mine_ref, chosen_ref,
     source_ref, total_ref, far_out, far_in, near_out, near_in,
     load_sem, spread_out, spread_in, slot_out, slot_in,
@@ -149,7 +149,7 @@
         pl.semaphore_signal(barrier, inc=1, device_id={"hour": to})
     load_table.start()
 
-    wanted_vec[...] = slot_table(lists_ref, counts_ref, padded_ref, blocks)
+    wanted_vec[...] = slot_table(lists_ref, padded_ref, blocks)
     load_wanted.start()
     band = band_matrix()
     load_x.wait()
@@ -162,7 +162,7 @@
 
     for kind in range(2):
         def spread(k, carry):
-            to = lax.rem(chip + k, chips)
+            to = lax.rem(chip + k * 9, chips)
 
             @pl.when((k > 0) | (core != kind))
             def _():
@@ -302,7 +302,7 @@
     return pl.pallas_call(
         functools.partial(fused_kernel, scale, blocks, hours),
         out_shape=jax.ShapeDtypeStruct((2, 2, rows, LAGS), jnp.float32),
-        in_specs=[vmem, vmem, leave, leave],
+        in_specs=[vmem, leave, leave],
         out_specs=vmem,
         scratch_shapes=[
             pltpu.VMEM(spectra.shape, bf16),
@@ -326,17 +326,16 @@
         compiler_params=pltpu.CompilerParams(
             collective_id=0, has_side_effects=True, vmem_limit_bytes=52 << 20
         ),
-    )(lists, counts[None], spectra, table)
-
-
-def slot_table(lists_ref, counts_ref, padded_ref, blocks):
-    most = lists_ref.shape[0]
+    )(jnp.concatenate([lists, counts[None]], 0), spectra, table)
+
+
+def slot_table(lists_ref, padded_ref, blocks):
+    most = lists_ref.shape[0] - 1
     shape = (blocks, 128)
     receiver = lax.broadcasted_iota(jnp.int32, shape, 0)
     lane = lax.broadcasted_iota(jnp.int32, shape, 1)
     padded_ref[...] = jnp.full(padded_ref.shape, -1, jnp.int32)
-    padded_ref[:most, :blocks] = lists_ref[...]
-    padded_ref[most:most + 1, :blocks] = counts_ref[...]
+    padded_ref[:most + 1, :blocks] = lists_ref[...]
     counts = jnp.broadcast_to(padded_ref[most:most + 1, :], shape)
     member = jnp.zeros(shape, jnp.int32)
     for offset in range(most):

time: 48 us -> 47.3 us (0.985)
  local copies, waits for them, and re-layouts: 2.31 us -> 0.97 us
  other arithmetic: 0 us -> 0.71 us
    unnamed x5 -> x1, local copies, waits for them, and re-layouts: 2.31 us -> 0.97 us
    concatenate x0 -> x1, other arithmetic: none -> 0.71 us  [fused(): jnp.concatenate([lists, counts[None]], 0)]
where the time goes in v7:
time: 47.3 us; the launch traced here: 47.2 us
  Pallas kernels  45.5 us (96%)
  local copies, waits for them, and re-layouts  0.97 us (2%)
  other arithmetic  0.71 us (2%)
    pallas_call x1, Pallas kernels, fused(): pl.pallas_call(functools.partial(fused_kernel, scale, blocks, hours), out...  45.5 us
    unnamed x1, local copies, waits for them, and re-layouts  0.97 us

profile of v7, /device:TPU:1, one launch (start us, length us, event | category | flops | bytes accessed | tf_op | source)
XLA Modules:
  0.0 47.2 jit_solution(2524585654876208545)
XLA Ops:
  0.0 0.7 %pad_add_fusion.lists_ref = s32[5,64]{1,0:T(8,128)S(1)} fusion(s32[1,64]{1,0:T(1,128)} %bitcast.5, s32[4,64]{1,0:T(4,128)} %bitcast.4), kind=kLoop, calls=%fused_computation | loop fusion | flops 320 | bytes 2560 | tf_op jit(solution)/shard_map/concatenate | solution.py:329
  0.7 45.5 %shard_map.46 = f32[2,2,256,256]{3,2,1,0:T(8,128)S(1)} custom-call(s32[5,64]{1,0:T(8,128)S(1)} %pad_add_fusion.lists_ref, bf16[2,2,128,2560]{3,2,1,0:T(8,128)(2,1)} %x_any.1, bf16[4,1280,256]{2,1,0:T(8,128)(2,1)} %constant.2.clone.table_any), custom_call_target="tpu_custom_call" | custom-call | tf_op jit(solution)/shard_map/pallas_call | solution.py:302
  46.2 1.0 %copy.6 = f32[1,8,128,256]{3,2,1,0:T(8,128)} copy(f32[1,8,128,256]{3,2,1,0:T(8,128)S(1)} %bitcast.3) | data formatting | bytes 2097152
